TPU v7x, 256 devices: a whole 4x4x8 slice. The times are simulated.
256 devices in a mesh: row: 16 (over z, core), col: 16 (over x, y).
Axes of the slice: x: 4, y: 4, z: 8, core: 2. Of those that a mesh axis runs over, the one named last changes fastest.
Arguments:
- matrix: float32 [12288, 12288], P('row', 'col'), may hold values from -40 to 40
Outputs:
- reduced: float32 [12288, 12288], P('row', 'col')
All inputs are finite; a program needn't handle non-finite values.
Results may differ from a plain program's by a relative error of at most 0.00013.
Values sent between devices are 32-bit elements; how exact they have to be, the bound alone decides.
A program may use at most 128 MiB of HBM per device.

v0:
```python
import functools

import jax
import jax.numpy as jnp
from jax import lax
from jax.experimental import pallas as pl
from jax.experimental.pallas import tpu as pltpu
from jax.sharding import PartitionSpec as P

BAND = 128
HIGH = lax.Precision.HIGHEST
VMEM = pltpu.VMEM
MESH = pl.DeviceIdType.MESH


def dot(left, right):
    return jnp.dot(left, right, precision=HIGH, preferred_element_type=jnp.float32)


def mm(left, right, ca=1, cb=0):
    return lax.dot_general(
        left, right, (((ca,), (cb,)), ((), ())), precision=HIGH, preferred_element_type=jnp.float32
    )


def eliminate(x_ref, jordan):
    n = x_ref.shape[0]
    lane = lax.broadcasted_iota(jnp.int32, (1, n), 1)
    rows = lax.broadcasted_iota(jnp.int32, (n, 1), 0)
    rows8 = lax.broadcasted_iota(jnp.int32, (8, 1), 0)

    def block(j, _):
        full = x_ref[...]
        strip = x_ref[pl.ds(pl.multiple_of(8 * j, 8), 8), :]
        for i in range(8):
            row = strip[i : i + 1, :]
            inv = 1.0 / row[:, i : i + 1]
            here = lane == i
            row = jnp.where(here, 1.0, row)

            def update(x, ids):
                col = x[:, i : i + 1] * inv
                if jordan:
                    pivot = ids == i
                    col = jnp.where(pivot, -inv, col)
                    return jnp.where(here | pivot, 0.0, x) - col * row
                below = ids > i
                col = jnp.where(below, col, 0.0)
                return jnp.where(here & below, 0.0, x) - col * row

            full = update(full, rows - 8 * j)
            strip = update(strip, rows8)
        x_ref[...] = pltpu.roll(full, n - 8, 1)
        return 0

    lax.fori_loop(0, n // 8, block, 0)


def piece(ref, k):
    parts, _, n = ref.shape
    rows = BAND // parts
    return ref[:, k * rows : (k + 1) * rows, :].reshape(BAND, n)


def factor_kernel(g_ref, t_ref, cinv_ref, rinv_ref, f_ref, ft_ref, finv_ref, finvt_ref):
    n = BAND
    r = lax.broadcasted_iota(jnp.int32, (n, n), 0)
    c = lax.broadcasted_iota(jnp.int32, (n, n), 1)
    eye = (r == c).astype(jnp.float32)
    cinv_ref[...] = piece(g_ref, 0)
    eliminate(cinv_ref, False)
    x = cinv_ref[...]
    diag = jnp.sum(jnp.where(r == c, x, 0.0), axis=1, keepdims=True)
    scale = 1.0 / jnp.sqrt(diag)
    cinv = jnp.where(r > c, x, eye) * scale
    cinv = jnp.where(r >= c, cinv, 0.0)
    cinv_ref[...] = cinv
    rinv_ref[...] = cinv.T
    f = dot(t_ref[...] if len(t_ref.shape) == 2 else piece(t_ref, 1), rinv_ref[...]) + eye
    f_ref[...] = f
    ft_ref[...] = f.T
    finv_ref[...] = f
    eliminate(finv_ref, True)
    finvt_ref[...] = finv_ref[...].T


def factor(gram, top):
    shape = jax.ShapeDtypeStruct((BAND, BAND), jnp.float32)
    return pl.pallas_call(
        factor_kernel,
        out_shape=(shape,) * 6,
        in_specs=[pl.BlockSpec(memory_space=VMEM)] * 2,
        out_specs=(pl.BlockSpec(memory_space=VMEM),) * 6,
        cost_estimate=pl.CostEstimate(flops=40_000_000, bytes_accessed=400_000_000, transcendentals=0),
        name="factor",
    )(gram, top)


def weights(fac, h, s_top, s_topt, a_ss):
    cinv, rinv, _, _, finv, finvt = fac
    half = dot(cinv, h) + s_top
    j = dot(half, rinv) + dot(cinv, s_topt) + a_ss
    return dot(dot(finv, j), finvt)


def step_one_kernel(
    pos_ref, cinv_ref, rinv_ref, f_ref, ft_ref, finv_ref, finvt_ref, h_ref, ht_ref, g_ref,
    pr_ref, sr_ref, pc_ref, sc_ref,
    left_ref, right_ref, p2r_ref, p2c_ref, e2r_ref, e2c_ref, t2_ref, a33_ref, small_ref,
):
    b = BAND
    n = pr_ref.shape[0]
    always = pos_ref[0] >= 0
    sums = lambda k: h_ref[k * b : (k + 1) * b, :]
    sumst = lambda k: ht_ref[:, k * b : (k + 1) * b]
    a22, a31, a32, a33, a13, a23 = (functools.partial(piece, g_ref, k) for k in range(2, 8))

    @pl.when(always)
    def _():
        fac = tuple(ref[...] for ref in (cinv_ref, rinv_ref, f_ref, ft_ref, finv_ref, finvt_ref))
        small_ref[0, :, :] = weights(fac, sums(0), sums(1), sumst(1), a22())

    @pl.when(always)
    def _():
        small_ref[6, :, :] = dot(a31(), rinv_ref[...])
        small_ref[3, :, :] = dot(cinv_ref[...], a13())

    def work(slot, house, sums, cols):
        @pl.when(always)
        def _():
            rows = dot(dot(sums, rinv_ref[...]) + cols(), finvt_ref[...])
            small_ref[slot, :, :] = rows - 0.5 * dot(house(), small_ref[0])

    def workt(slot, house, sums, cols):
        @pl.when(always)
        def _():
            rows = dot(finv_ref[...], dot(cinv_ref[...], sums) + cols())
            small_ref[slot, :, :] = rows - 0.5 * dot(small_ref[0], house())

    work(5, lambda: small_ref[6], sums(2), a32)
    work(4, lambda: f_ref[...], sums(1), a22)
    workt(1, lambda: ft_ref[...], sumst(1), a22)
    workt(2, lambda: small_ref[3], sumst(2), a23)

    @pl.when(always)
    def _():
        t2_ref[...] = a32() - dot(small_ref[6], small_ref[1]) - dot(small_ref[5], ft_ref[...])
        a33_ref[...] = a33() - dot(small_ref[6], small_ref[2]) - dot(small_ref[5], small_ref[3])

    tile = 2 * b if n % (2 * b) == 0 else b

    def side(start, p_ref, s_ref, out_ref, house_at, work_at, p2_ref, e2_ref):
        @pl.loop(0, n // tile)
        def _(step):
            at = pl.ds(pl.multiple_of(step * tile, tile), tile)
            ids = start * n + step * tile + lax.broadcasted_iota(jnp.int32, (tile, b), 0)
            lane = lax.broadcasted_iota(jnp.int32, (tile, b), 1)
            panel = jnp.where(ids >= b, p_ref[at, 0:b], 0.0)
            house = dot(panel, rinv_ref[...]) + (ids - b == lane).astype(jnp.float32)
            cols = p_ref[at, b : 2 * b]
            wk = dot(dot(s_ref[at, :], rinv_ref[...]) + cols, finvt_ref[...]) - 0.5 * dot(house, small_ref[0])
            out_ref[at, house_at : house_at + b] = house
            out_ref[at, work_at : work_at + b] = wk
            p2 = cols - dot(house, small_ref[1]) - dot(wk, ft_ref[...])
            p2_ref[at, :] = jnp.where(ids >= 2 * b, p2, 0.0)
            e2_ref[at, :] = p_ref[at, 2 * b : 3 * b] - dot(house, small_ref[2]) - dot(wk, small_ref[3])

    side(pos_ref[0], pr_ref, sr_ref, left_ref, 0, b, p2r_ref, e2r_ref)
    side(pos_ref[1], pc_ref, sc_ref, right_ref, b, 0, p2c_ref, e2c_ref)


def step_two_kernel(
    pos_ref, cinv_ref, rinv_ref, f_ref, ft_ref, finv_ref, finvt_ref, h_ref, ht_ref, a33_ref,
    pr_ref, sr_ref, er_ref, pc_ref, sc_ref, ec_ref,
    left_ref, right_ref, z_ref,
):
    b = BAND
    n = pr_ref.shape[0]
    tile = 2 * b if n % (2 * b) == 0 else b

    @pl.when(pos_ref[0] >= 0)
    def _():
        fac = tuple(ref[...] for ref in (cinv_ref, rinv_ref, f_ref, ft_ref, finv_ref, finvt_ref))
        z_ref[...] = weights(fac, h_ref[0:b, :], h_ref[b : 2 * b, :], ht_ref[:, b : 2 * b], a33_ref[...])

    def side(start, p_ref, s_ref, e_ref, out_ref, house_at, work_at):
        @pl.loop(0, n // tile)
        def _(step):
            at = pl.ds(pl.multiple_of(step * tile, tile), tile)
            ids = start * n + step * tile + lax.broadcasted_iota(jnp.int32, (tile, b), 0)
            lane = lax.broadcasted_iota(jnp.int32, (tile, b), 1)
            house = dot(p_ref[at, :], rinv_ref[...]) + (ids - 2 * b == lane).astype(jnp.float32)
            out_ref[at, house_at : house_at + b] = house
            ay = dot(s_ref[at, :], rinv_ref[...]) + e_ref[at, :]
            out_ref[at, work_at : work_at + b] = dot(ay, finvt_ref[...]) - 0.5 * dot(house, z_ref[...])

    side(pos_ref[0], pr_ref, sr_ref, er_ref, left_ref, 0, b)
    side(pos_ref[1], pc_ref, sc_ref, ec_ref, right_ref, b, 0)


def call(body, outs, name, scratch=()):
    def run(pos, *args):
        return pl.pallas_call(
            body,
            out_shape=tuple(jax.ShapeDtypeStruct(s, jnp.float32) for s in outs),
            in_specs=[pl.BlockSpec(memory_space=pltpu.SMEM)] + [pl.BlockSpec(memory_space=VMEM)] * len(args),
            out_specs=(pl.BlockSpec(memory_space=VMEM),) * len(outs),
            scratch_shapes=scratch,
            name=name,
        )(pos, *args)

    return run


def greet(nr, nc):
    r, c = lax.axis_index("row"), lax.axis_index("col")
    barrier = pltpu.get_barrier_semaphore()
    for k in range(1, nc):
        pl.semaphore_signal(barrier, inc=1, device_id=(r, (c + k) % nc), device_id_type=MESH)
    for k in range(1, nr):
        pl.semaphore_signal(barrier, inc=1, device_id=((r + k) % nr, c), device_id_type=MESH)
    pl.semaphore_wait(barrier, nr + nc - 2)
    return r, c


def rows_at(index, size):
    return pl.ds(pl.multiple_of(index * size, 8), size)


def spread_kernel(nr, nc, xr, xc, pr, pc, root_send, root_recv, send, recv):
    r, c = greet(nr, nc)
    sides = (
        (0, nc, c, xr, pr, lambda k: (r, k)),
        (1, nr, r, xc, pc, lambda k: (k, c)),
    )

    def scatter(side, size, src, dst, dev, k):
        return pltpu.make_async_remote_copy(
            src_ref=src.at[pl.ds(k * size, size)],
            dst_ref=dst.at[pl.ds(k * size, size)],
            send_sem=root_send.at[side, k],
            recv_sem=root_recv.at[side],
            device_id=dev(k),
            device_id_type=MESH,
        )

    for side, parts, me, src, dst, dev in sides:
        size = src.shape[0] // parts

        @pl.when(me == 0)
        def _():
            for k in range(1, parts):
                scatter(side, size, src, dst, dev, k).start()
            dst[0:size, :] = src[0:size, :]

    copies = []
    for side, parts, me, src, dst, dev in sides:
        size = src.shape[0] // parts

        @pl.when(me != 0)
        def _():
            scatter(side, size, src, dst, dev, 1).wait_recv()

        for k in range(1, parts):
            copy = pltpu.make_async_remote_copy(
                src_ref=dst.at[rows_at(me, size)],
                dst_ref=dst.at[rows_at(me, size)],
                send_sem=send.at[side, k],
                recv_sem=recv.at[side, k],
                device_id=dev((me + k) % parts),
                device_id_type=MESH,
            )
            copy.start()
            copies.append(copy)
    for copy in copies:
        copy.wait()
    for side, parts, me, src, dst, dev in sides:
        size = src.shape[0] // parts

        @pl.when(me == 0)
        def _():
            for k in range(1, parts):
                scatter(side, size, src, dst, dev, k).wait_send()


def reduce_kernel(
    nr, nc, sr, sc, h, g, out_r, out_c, out_h, out_g,
    part_r, part_c, part_h, part_g, sum_r, sum_c, sum_h, sum_g, cols_h, all_h, send, recv,
):
    r, c = greet(nr, nc)
    size_r, size_c, size_h = sr.shape[0] // nc, sc.shape[0] // nr, h.shape[0] // nc

    def along(axis, phase, source, target):
        parts, me = (nc, c) if axis == "col" else (nr, r)
        copies = []
        for k in range(1, parts):
            to = (me + k) % parts
            copy = pltpu.make_async_remote_copy(
                src_ref=source(to),
                dst_ref=target(k),
                send_sem=send.at[phase, k],
                recv_sem=recv.at[phase, k],
                device_id=(r, to) if axis == "col" else (to, c),
                device_id_type=MESH,
            )
            copy.start()
            copies.append(copy)
        return copies

    def finish(copies):
        for copy in copies:
            copy.wait()

    g_copies = along("row", 0, lambda to: g, lambda k: part_g.at[r])
    h_copies = along("col", 1, lambda to: h.at[rows_at(to, size_h)], lambda k: part_h.at[k])
    r_copies = along("col", 2, lambda to: sr.at[rows_at(to, size_r)], lambda k: part_r.at[k])
    c_copies = along("row", 3, lambda to: sc.at[rows_at(to, size_c)], lambda k: part_c.at[k])
    part_g[r] = g[...]

    def add(parts, count, start):
        value = start
        for k in range(count):
            value = parts[k] if value is None else value + parts[k]
        return value

    finish(g_copies)
    value = add(part_g, nr, None)
    sum_g[...] = value
    out_g[c] = value
    g_copies = along("col", 4, lambda to: sum_g, lambda k: out_g.at[c])

    finish(h_copies)
    value = h[rows_at(c, size_h), :]
    for k in range(1, nc):
        value = value + part_h[k]
    sum_h[...] = value
    cols_h[r] = value
    h_copies = along("row", 5, lambda to: sum_h, lambda k: cols_h.at[r])

    finish(r_copies)
    value = sr[rows_at(c, size_r), :]
    for k in range(1, nc):
        value = value + part_r[k]
    sum_r[...] = value
    out_r[rows_at(c, size_r), :] = value
    r_copies = along("col", 6, lambda to: sum_r, lambda k: out_r.at[rows_at(c, size_r)])

    finish(c_copies)
    value = sc[rows_at(r, size_c), :]
    for k in range(1, nr):
        value = value + part_c[k]
    sum_c[...] = value
    out_c[rows_at(r, size_c), :] = value
    c_copies = along("row", 7, lambda to: sum_c, lambda k: out_c.at[rows_at(r, size_c)])

    finish(h_copies)
    value = add(cols_h, nr, None)
    all_h[...] = value
    out_h[rows_at(c, size_h), :] = value
    h_copies = along("col", 8, lambda to: all_h, lambda k: out_h.at[rows_at(c, size_h)])
    for copies in (g_copies, r_copies, c_copies, h_copies):
        finish(copies)


def spread(nr, nc, xr, xc):
    most = max(nr, nc)
    dma = pltpu.SemaphoreType.DMA
    return pl.pallas_call(
        functools.partial(spread_kernel, nr, nc),
        out_shape=tuple(jax.ShapeDtypeStruct(x.shape, jnp.float32) for x in (xr, xc)),
        in_specs=[pl.BlockSpec(memory_space=VMEM)] * 2,
        out_specs=(pl.BlockSpec(memory_space=VMEM),) * 2,
        scratch_shapes=[dma((2, most)), dma((2,)), dma((2, most)), dma((2, most))],
        compiler_params=pltpu.CompilerParams(collective_id=0, has_side_effects=True),
        name="spread",
    )(xr, xc)


def reduce(nr, nc, sr, sc, h, g, which):
    most = max(nr, nc)
    dma = pltpu.SemaphoreType.DMA
    b = sr.shape[1]
    size_r, size_c, size_h, size_g = sr.shape[0] // nc, sc.shape[0] // nr, h.shape[0] // nc, g.shape[0]
    outs = (sr.shape, sc.shape, h.shape, (nc, size_g, b))
    scratch = [
        (nc, size_r, b), (nr, size_c, b), (nc, size_h, b), (nr, size_g, b),
        (size_r, b), (size_c, b), (size_h, b), (size_g, b), (nr, size_h, b), (size_h, b),
    ]
    return pl.pallas_call(
        functools.partial(reduce_kernel, nr, nc),
        out_shape=tuple(jax.ShapeDtypeStruct(s, jnp.float32) for s in outs),
        in_specs=[pl.BlockSpec(memory_space=VMEM)] * 4,
        out_specs=(pl.BlockSpec(memory_space=VMEM),) * 4,
        scratch_shapes=[VMEM(s, jnp.float32) for s in scratch] + [dma((9, most)), dma((9, most))],
        compiler_params=pltpu.CompilerParams(collective_id=which, has_side_effects=True),
        name=f"reduce_{which}",
    )(sr, sc, h, g)


def shards(nr, nc, matrix):
    n = matrix.shape[0]
    b = BAND
    row, col = lax.axis_index("row"), lax.axis_index("col")
    pos = jnp.stack([row, col]).astype(jnp.int32)
    row_ids = row * n + jnp.arange(n, dtype=jnp.int32)
    col_ids = col * n + jnp.arange(n, dtype=jnp.int32)

    def slices(blocks):
        size = b // nc
        picked = lax.dynamic_slice_in_dim(jnp.stack(blocks), col * size, size, 1)
        return picked.reshape(len(blocks) * size, b)

    def products(current, rows, cols, first, last):
        sr = mm(current, cols)
        sc = mm(current, rows, 0, 0)
        head = jnp.where(row == 0, sr[first * b : last * b], 0.0)
        return sr, sc, jnp.concatenate([mm(rows, sr, 0, 0), head], 0)

    pr, pc = spread(nr, nc, matrix[:, : 3 * b], matrix[: 3 * b, :].T)
    p1r = jnp.where(row_ids[:, None] >= b, pr[:, :b], 0.0)
    p1c = jnp.where(col_ids[:, None] >= b, pc[:, :b], 0.0)
    corner = jnp.where(row == 0, pr[: 3 * b], 0.0)
    where = ((1, 0), (1, 1), (2, 0), (2, 1), (2, 2), (0, 2), (1, 2))
    tops = [corner[i * b : (i + 1) * b, j * b : (j + 1) * b] for i, j in where]
    g = slices([mm(p1r, p1r, 0, 0), *tops])
    sr, sc, h, g = reduce(nr, nc, *products(matrix, p1r, p1c, 1, 3), g, 1)
    fac = factor(g, g)
    one = call(
        step_one_kernel,
        [(n, 2 * b), (n, 2 * b), (n, b), (n, b), (n, b), (n, b), (b, b), (b, b)],
        "step_one",
        [VMEM((7, b, b), jnp.float32)],
    )
    left, right, p2r, p2c, e2r, e2c, t2, a33 = one(pos, *fac, h, h.T, g, pr, sr, pc, sc)
    updated = matrix - mm(left, right, 1, 1)
    sr2, sc2, h2, g2 = reduce(nr, nc, *products(updated, p2r, p2c, 2, 3), slices([mm(p2r, p2r, 0, 0)]), 2)
    fac2 = factor(g2, t2)
    two = call(step_two_kernel, [(n, 2 * b), (n, 2 * b)], "step_two", [VMEM((b, b), jnp.float32)])
    left2, right2 = two(pos, *fac2, h2, h2.T, a33, p2r, sr2, e2r, p2c, sc2, e2c)
    return updated - mm(left2, right2, 1, 1)


def solution(mesh):
    spec = P("row", "col")
    body = functools.partial(shards, mesh.shape["row"], mesh.shape["col"])
    return jax.shard_map(body, mesh=mesh, in_specs=(spec,), out_specs=spec, check_vma=False)
```

profile of v0, /device:TPU:1, one launch (start us, length us, event | category | flops | bytes accessed | tf_op | source)
XLA Modules:
  0.0 254.4 jit_solution(256929089854617761)
XLA Ops:
  0.0 0.0 slice-start
  0.0 0.7 pad_add_fusion.pos_ref
  0.7 0.0 copy-start
  0.7 0.6 slice-done
  1.3 1.4 copy.8
  2.7 0.0 copy-done
  2.7 1.1 slice.42.xr
  3.8 57.3 %spread.1 = (f32[768,384]{1,0:T(8,128)}, f32[768,384]{1,0:T(8,128)}) custom-call(f32[768,384]{1,0:T(8,128)} %slice.42.xr, f32[768,384]{1,0:T(8,128)} %bitcast.57), custom_call_target="tpu_custom_call" | custom-call | tf_op jit(solution)/shard_map/spread/pallas_call | solution.py:368
  61.0 0.0 copy-start.2
  61.1 3.3 %fusion.1 = f32[128,768]{1,0:T(8,128)S(1)} fusion(f32[768,768]{1,0:T(8,128)S(1)} %copy-done, f32[768,384]{1,0:T(8,128)} %get-tuple-element.37.pc_ref, pred[768]{0:T(1024)(128)(4,1)S(1)} %add_compare_fusion.1), kind=kOutput, calls=%fused_computation.7 | convolution fusion | flops 906067968 | bytes 3146496 | tf_op jit(solution)/shard_map/dot_general | solution.py:21
  64.4 0.0 copy-start.4
  64.4 0.7 copy-done.4
  65.2 0.0 copy-done.2
  65.2 1.5 fusion.4
  66.7 1.9 copy.3
  68.6 0.9 slice_select_fusion.5
  69.5 1.5 pad_maximum_fusion.h
  71.1 4.7 %convolution_bitcast_fusion.sc = f32[768,128]{1,0:T(8,128)} fusion(f32[768,768]{1,0:T(8,128)S(1)} %copy-done, f32[768,384]{1,0:T(8,128)S(1)} %copy-done.2, pred[768]{0:T(1024)(128)(4,1)S(1)} %add_compare_fusion), kind=kOutput, calls=%fused_computation.2 | convolution fusion | flops 906067968 | bytes 3146752 | tf_op jit(solution)/shard_map/dot_general | solution.py:21
  75.8 1.0 fusion
  77.0 0.6 dynamic-slice_bitcast_fusion.g
  77.6 47.6 %reduce_1.1 = (f32[768,128]{1,0:T(8,128)}, f32[768,128]{1,0:T(8,128)}, f32[384,128]{1,0:T(8,128)}, f32[16,64,128]{2,1,0:T(8,128)}) custom-call(f32[768,128]{1,0:T(8,128)} %bitcast.59, f32[768,128]{1,0:T(8,128)} %convolution_bitcast_fusion.sc, f32[384,128]{1,0:T(8,128)} %pad_maximum_fusion.h, f32[64,128]{1,0:T(8,128)} %dynamic-slice_bitcast_fusion.g), custom_call_target="tpu_custom_call" | custom-call | tf_op jit(solution)/shard_map/reduce_1/pallas_call | solution.py:389
  125.2 1.7 copy.5
  126.9 25.7 %factor.2 = (f32[128,128]{1,0:T(8,128)}, f32[128,128]{1,0:T(8,128)}, f32[128,128]{1,0:T(8,128)}, f32[128,128]{1,0:T(8,128)}, f32[128,128]{1,0:T(8,128)}, /*index=5*/f32[128,128]{1,0:T(8,128)}) custom-call(f32[16,64,128]{2,1,0:T(8,128)} %get-tuple-element.39.g_ref.t_ref, f32[16,64,128]{2,1,0:T(8,128)} %get-tuple-element.39.g_ref.t_ref), custom_call_target="tpu_custom_call" | custom-call | flops 40000000 | bytes 400000000 | tf_op jit(solution)/shard_map/factor/pallas_call | solution.py:89
  152.6 13.5 %step_one.1 = (f32[768,256]{1,0:T(8,128)}, f32[768,256]{1,0:T(8,128)}, f32[768,128]{1,0:T(8,128)}, f32[768,128]{1,0:T(8,128)}, f32[768,128]{1,0:T(8,128)}, /*ind...) custom-call(s32[2]{0:T(128)} %pad_add_fusion.pos_ref, f32[128,128]{1,0:T(8,128)} %get-tuple-element.40.cinv_ref, ...), custom_call_target="tpu_custom_call" | custom-call | tf_op jit(solution)/shard_map/step_one/pallas_call | solution.py:203
  166.1 1.9 fusion.27
  168.0 0.6 constant_dynamic-slice_fusion.g
  168.6 0.0 copy-start.5
  168.6 4.3 %convolution_subtract_fusion.1 = f32[768,768]{1,0:T(8,128)S(1)} fusion(f32[768,768]{1,0:T(8,128)} %param.1, f32[768,256]{1,0:T(8,128)} %get-tuple-element.49, f32[768,256]{1,0:T(8,128)} %get-tuple-element.50), kind=kOutput, calls=%fused_computation.1 | convolution fusion | flops 1812529152 | bytes 6291456 | tf_op jit(solution)/shard_map/dot_general | solution.py:21
  172.9 0.0 copy-done.5
  172.9 0.0 copy-start.1
  172.9 2.0 fusion.24.sr
  174.9 0.0 copy-start.3
  174.9 0.0 copy-done.1
  174.9 0.8 fusion.26
  175.7 0.7 pad_maximum_fusion.1.h
  176.4 4.6 %fusion.25.sc = f32[768,128]{1,0:T(8,128)} fusion(f32[768,768]{1,0:T(8,128)S(1)} %convolution_subtract_fusion.1, f32[768,128]{1,0:T(8,128)S(1)} %copy-done.1), kind=kOutput, calls=%fused_computation.47 | convolution fusion | flops 905969664 | bytes 3145728 | tf_op jit(solution)/shard_map/dot_general | solution.py:21
  181.0 0.0 copy-done.3
  181.0 33.6 %reduce_2.1 = (f32[768,128]{1,0:T(8,128)}, f32[768,128]{1,0:T(8,128)}, f32[256,128]{1,0:T(8,128)}, f32[16,8,128]{2,1,0:T(8,128)}) custom-call(f32[768,128]{1,0:T(8,128)} %copy-done.3, f32[768,128]{1,0:T(8,128)} %fusion.25.sc, f32[256,128]{1,0:T(8,128)} %pad_maximum_fusion.1.h, f32[8,128]{1,0:T(8,128)} %constant_dynamic-slice_fusion.g), custom_call_target="tpu_custom_call" | custom-call | tf_op jit(solution)/shard_map/reduce_2/pallas_call | solution.py:389
  214.6 1.7 copy.6
  216.3 25.5 %factor.3 = (f32[128,128]{1,0:T(8,128)}, f32[128,128]{1,0:T(8,128)}, f32[128,128]{1,0:T(8,128)}, f32[128,128]{1,0:T(8,128)}, f32[128,128]{1,0:T(8,128)}, /*index=5*/f32[128,128]{1,0:T(8,128)}) custom-call(f32[16,8,128]{2,1,0:T(8,128)} %get-tuple-element.53.g_ref, f32[128,128]{1,0:T(8,128)} %get-tuple-element.54.t_ref), custom_call_target="tpu_custom_call" | custom-call | flops 40000000 | bytes 400000000 | tf_op jit(solution)/shard_map/factor/pallas_call | solution.py:89
  241.8 7.7 %step_two.1 = (f32[768,256]{1,0:T(8,128)}, f32[768,256]{1,0:T(8,128)}) custom-call(s32[2]{0:T(128)} %pad_add_fusion.pos_ref, f32[128,128]{1,0:T(8,128)} %get-tuple-element.55.cinv_ref, f32[128,128]{1,0:T(8,128)} %get-tuple-element.56.rinv_ref, f32[128,128]{1,0:T(8,128)} %get-tuple-element.57.f_ref, f32[128,128]{1,0:T(8,128)} %get-tuple-element.58.ft_ref, ...), custom_call_target="tpu_custom_call" | custom-call | tf_op jit(solution)/shard_map/step_two/pallas_call | solution.py:203
  249.5 4.9 %convolution_subtract_fusion = f32[768,768]{1,0:T(8,128)} fusion(f32[768,768]{1,0:T(8,128)S(1)} %convolution_subtract_fusion.1, f32[768,256]{1,0:T(8,128)} %get-tuple-element.67, f32[768,256]{1,0:T(8,128)} %get-tuple-element.68), kind=kOutput, calls=%fused_computation | convolution fusion | flops 1812529152 | bytes 6291456 | tf_op jit(solution)/shard_map/dot_general | solution.py:21
  (11 shorter events, 0.1 us)
Async XLA Ops:
  0.0 1.3 slice-start
  0.7 2.0 copy-start
  61.0 4.1 %copy-start.2 = (f32[768,384]{1,0:T(8,128)S(1)}, f32[768,384]{1,0:T(8,128)}, u32[]{:S(2)}) copy-start(f32[768,384]{1,0:T(8,128)} %get-tuple-element.38.pr_ref) | copy-start | bytes 3538948
  64.4 0.7 copy-start.4
  168.6 4.3 %copy-start.5 = (f32[768,128]{1,0:T(8,128)S(1)}, f32[768,128]{1,0:T(8,128)}, u32[]{:S(2)}) copy-start(f32[768,128]{1,0:T(8,128)} %get-tuple-element.51.pc_ref) | copy-start | bytes 1179652
  172.9 2.0 copy-start.1
  174.9 6.1 %copy-start.3 = (f32[768,128]{1,0:T(8,128)}, f32[768,128]{1,0:T(8,128)S(1)}, u32[]{:S(2)}) copy-start(f32[768,128]{1,0:T(8,128)S(1)} %fusion.24.sr) | copy-start | bytes 1179652
where the time goes:
time: 255 us; the launch traced here: 254 us
  Pallas kernels  211 us (83%)
  matrix products  29.1 us (11%)
  local copies, waits for them, and re-layouts  10.4 us (4%)
  other arithmetic  3.84 us (2%)
    pallas_call x2, Pallas kernels, reduce(): pl.pallas_call(functools.partial(reduce_kernel, nr, nc), out_shape=tuple(...  81.2 us
    pallas_call x1, Pallas kernels, spread(): pl.pallas_call(functools.partial(spread_kernel, nr, nc), out_shape=tuple(...  57.3 us
    pallas_call x2, Pallas kernels, factor(): pl.pallas_call(factor_kernel, out_shape=(shape,) * 6, in_specs=[pl.BlockS...  51.2 us
    dot_general x10, matrix products, mm(): lax.dot_general(left, right, (((ca,), (cb,)), ((), ())), precision=HIGH,...  29.1 us
    pallas_call x2, Pallas kernels, run(): pl.pallas_call(body, out_shape=tuple((jax.ShapeDtypeStruct(s, jnp.float32...  21.2 us

commit v1 on v0

v1 whole, which is shorter than its diff:
```python
import functools

import jax
import jax.numpy as jnp
from jax import lax
from jax.experimental import pallas as pl
from jax.experimental.pallas import tpu as pltpu
from jax.sharding import PartitionSpec as P

BAND = 128
HIGH = lax.Precision.HIGHEST
VMEM = pltpu.VMEM
MESH = pl.DeviceIdType.MESH


def dot(left, right):
    return jnp.dot(left, right, precision=HIGH, preferred_element_type=jnp.float32)


def mm(left, right, ca=1, cb=0):
    return lax.dot_general(
        left, right, (((ca,), (cb,)), ((), ())), precision=HIGH, preferred_element_type=jnp.float32
    )


def eliminate(x_ref, jordan):
    n = x_ref.shape[0]
    lane = lax.broadcasted_iota(jnp.int32, (1, n), 1)
    rows = lax.broadcasted_iota(jnp.int32, (n, 1), 0)
    rows8 = lax.broadcasted_iota(jnp.int32, (8, 1), 0)

    def block(j, _):
        full = x_ref[...]
        strip = x_ref[pl.ds(pl.multiple_of(8 * j, 8), 8), :]
        for i in range(8):
            row = strip[i : i + 1, :]
            inv = 1.0 / row[:, i : i + 1]
            here = lane == i
            row = jnp.where(here, 1.0, row)

            def update(x, ids):
                col = x[:, i : i + 1] * inv
                if jordan:
                    pivot = ids == i
                    col = jnp.where(pivot, -inv, col)
                    return jnp.where(here | pivot, 0.0, x) - col * row
                below = ids > i
                col = jnp.where(below, col, 0.0)
                return jnp.where(here & below, 0.0, x) - col * row

            full = update(full, rows - 8 * j)
            strip = update(strip, rows8)
        x_ref[...] = pltpu.roll(full, n - 8, 1)
        return 0

    lax.fori_loop(0, n // 8, block, 0)


def piece(ref, k):
    parts, _, n = ref.shape
    rows = BAND // parts
    return ref[:, k * rows : (k + 1) * rows, :].reshape(BAND, n)


def whole(ref):
    parts, rows, n = ref.shape
    return ref[...].reshape(parts * rows, n)


def invert_chol(gram, cinv_ref, rinv_ref):
    n = BAND
    r = lax.broadcasted_iota(jnp.int32, (n, n), 0)
    c = lax.broadcasted_iota(jnp.int32, (n, n), 1)
    cinv_ref[...] = gram
    eliminate(cinv_ref, False)
    x = cinv_ref[...]
    diag = jnp.sum(jnp.where(r == c, x, 0.0), axis=1, keepdims=True)
    cinv = jnp.where(r > c, x, (r == c).astype(jnp.float32)) / jnp.sqrt(diag)
    cinv_ref[...] = cinv
    rinv_ref[...] = cinv.T


def invert_top(top, rinv_ref, f_ref, ft_ref, finv_ref, finvt_ref):
    n = BAND
    r = lax.broadcasted_iota(jnp.int32, (n, n), 0)
    c = lax.broadcasted_iota(jnp.int32, (n, n), 1)
    f = dot(top, rinv_ref[...]) + (r == c).astype(jnp.float32)
    f_ref[...] = f
    ft_ref[...] = f.T
    finv_ref[...] = f
    eliminate(finv_ref, True)
    finvt_ref[...] = finv_ref[...].T


def weights(fac, h, s_top, s_topt, a_ss):
    cinv, rinv, _, _, finv, finvt = fac
    half = dot(cinv, h) + s_top
    j = dot(half, rinv) + dot(cinv, s_topt) + a_ss
    return dot(dot(finv, j), finvt)


def step_one_kernel(
    pos_ref, cinv_ref, rinv_ref, f_ref, ft_ref, finv_ref, finvt_ref, h_ref, ht_ref, g_ref,
    pr_ref, sr_ref, er_ref, pc_ref, sc_ref, ec_ref,
    left_ref, right_ref, p2r_ref, p2c_ref, t2_ref, a33_ref, small_ref,
):
    b = BAND
    n = pr_ref.shape[0]
    always = pos_ref[0] >= 0
    sums = lambda k: h_ref[k * b : (k + 1) * b, :]
    sumst = lambda k: ht_ref[:, k * b : (k + 1) * b]
    a22, a31, a32, a33, a13, a23 = (functools.partial(piece, g_ref, k) for k in range(1, 7))

    @pl.when(always)
    def _():
        fac = tuple(ref[...] for ref in (cinv_ref, rinv_ref, f_ref, ft_ref, finv_ref, finvt_ref))
        small_ref[0, :, :] = weights(fac, sums(0), sums(1), sumst(1), a22())

    @pl.when(always)
    def _():
        small_ref[6, :, :] = dot(a31(), rinv_ref[...])
        small_ref[3, :, :] = dot(cinv_ref[...], a13())

    def work(slot, house, sums, cols):
        @pl.when(always)
        def _():
            rows = dot(dot(sums, rinv_ref[...]) + cols(), finvt_ref[...])
            small_ref[slot, :, :] = rows - 0.5 * dot(house(), small_ref[0])

    def workt(slot, house, sums, cols):
        @pl.when(always)
        def _():
            rows = dot(finv_ref[...], dot(cinv_ref[...], sums) + cols())
            small_ref[slot, :, :] = rows - 0.5 * dot(small_ref[0], house())

    work(5, lambda: small_ref[6], sums(2), a32)
    work(4, lambda: f_ref[...], sums(1), a22)
    workt(1, lambda: ft_ref[...], sumst(1), a22)
    workt(2, lambda: small_ref[3], sumst(2), a23)

    @pl.when(always)
    def _():
        t2_ref[...] = a32() - dot(small_ref[6], small_ref[1]) - dot(small_ref[5], ft_ref[...])
        a33_ref[...] = a33() - dot(small_ref[6], small_ref[2]) - dot(small_ref[5], small_ref[3])

    tile = 2 * b if n % (2 * b) == 0 else b

    def side(start, p_ref, s_ref, e_ref, out_ref, house_at, work_at, p2_ref):
        @pl.loop(0, n // tile)
        def _(step):
            at = pl.ds(pl.multiple_of(step * tile, tile), tile)
            ids = start * n + step * tile + lax.broadcasted_iota(jnp.int32, (tile, b), 0)
            lane = lax.broadcasted_iota(jnp.int32, (tile, b), 1)
            house = dot(p_ref[at, :], rinv_ref[...]) + (ids - b == lane).astype(jnp.float32)
            cols = e_ref[at, :]
            wk = dot(dot(s_ref[at, :], rinv_ref[...]) + cols, finvt_ref[...]) - 0.5 * dot(house, small_ref[0])
            out_ref[at, house_at : house_at + b] = house
            out_ref[at, work_at : work_at + b] = wk
            p2 = cols - dot(house, small_ref[1]) - dot(wk, ft_ref[...])
            p2_ref[at, :] = jnp.where(ids >= 2 * b, p2, 0.0)

    side(pos_ref[0], pr_ref, sr_ref, er_ref, left_ref, 0, b, p2r_ref)
    side(pos_ref[1], pc_ref, sc_ref, ec_ref, right_ref, b, 0, p2c_ref)


def step_two_kernel(
    pos_ref, cinv_ref, rinv_ref, f_ref, ft_ref, finv_ref, finvt_ref, h_ref, ht_ref, a33_ref,
    pr_ref, sr_ref, er_ref, pc_ref, sc_ref, ec_ref,
    left_ref, right_ref, z_ref,
):
    b = BAND
    n = pr_ref.shape[0]
    tile = 2 * b if n % (2 * b) == 0 else b

    @pl.when(pos_ref[0] >= 0)
    def _():
        fac = tuple(ref[...] for ref in (cinv_ref, rinv_ref, f_ref, ft_ref, finv_ref, finvt_ref))
        z_ref[...] = weights(fac, h_ref[0:b, :], h_ref[b : 2 * b, :], ht_ref[:, b : 2 * b], a33_ref[...])

    def side(start, p_ref, s_ref, e_ref, out_ref, house_at, work_at):
        @pl.loop(0, n // tile)
        def _(step):
            at = pl.ds(pl.multiple_of(step * tile, tile), tile)
            ids = start * n + step * tile + lax.broadcasted_iota(jnp.int32, (tile, b), 0)
            lane = lax.broadcasted_iota(jnp.int32, (tile, b), 1)
            house = dot(p_ref[at, :], rinv_ref[...]) + (ids - 2 * b == lane).astype(jnp.float32)
            out_ref[at, house_at : house_at + b] = house
            ay = dot(s_ref[at, :], rinv_ref[...]) + e_ref[at, :]
            out_ref[at, work_at : work_at + b] = dot(ay, finvt_ref[...]) - 0.5 * dot(house, z_ref[...])

    side(pos_ref[0], pr_ref, sr_ref, er_ref, left_ref, 0, b)
    side(pos_ref[1], pc_ref, sc_ref, ec_ref, right_ref, b, 0)


def call(body, outs, name, scratch=()):
    def run(pos, *args):
        return pl.pallas_call(
            body,
            out_shape=tuple(jax.ShapeDtypeStruct(s, jnp.float32) for s in outs),
            in_specs=[pl.BlockSpec(memory_space=pltpu.SMEM)] + [pl.BlockSpec(memory_space=VMEM)] * len(args),
            out_specs=(pl.BlockSpec(memory_space=VMEM),) * len(outs),
            scratch_shapes=scratch,
            name=name,
        )(pos, *args)

    return run


def greet(nr, nc):
    r, c = lax.axis_index("row"), lax.axis_index("col")
    barrier = pltpu.get_barrier_semaphore()
    for k in range(1, nc):
        pl.semaphore_signal(barrier, inc=1, device_id=(r, (c + k) % nc), device_id_type=MESH)
    for k in range(1, nr):
        pl.semaphore_signal(barrier, inc=1, device_id=((r + k) % nr, c), device_id_type=MESH)
    pl.semaphore_wait(barrier, nr + nc - 2)
    return r, c


def rows_at(index, size):
    return pl.ds(pl.multiple_of(index * size, 8), size)


class Spread:
    def __init__(self, axis, parts, me, other, dst, sems):
        self.axis, self.parts, self.me, self.other, self.dst = axis, parts, me, other, dst
        self.root_send, self.root_recv, self.send, self.recv = sems
        self.size = dst.shape[0] // parts

    def device(self, k):
        return (self.other, k) if self.axis == "col" else (k, self.other)

    def copy(self, k, src):
        rows = pl.ds(k * self.size, self.size)
        return pltpu.make_async_remote_copy(
            src_ref=src(rows),
            dst_ref=self.dst.at[rows],
            send_sem=self.root_send.at[k],
            recv_sem=self.root_recv,
            device_id=self.device(k),
            device_id_type=MESH,
        )

    def scatter(self, src):
        @pl.when(self.me == 0)
        def _():
            for k in range(1, self.parts):
                self.copy(k, src).start()
            rows = pl.ds(0, self.size)
            self.dst[rows, :] = src(rows)[...]

    def gather(self, src):
        @pl.when(self.me != 0)
        def _():
            self.copy(1, src).wait_recv()

        self.copies = []
        for k in range(1, self.parts):
            rows = rows_at(self.me, self.size)
            copy = pltpu.make_async_remote_copy(
                src_ref=self.dst.at[rows],
                dst_ref=self.dst.at[rows],
                send_sem=self.send.at[k],
                recv_sem=self.recv.at[k],
                device_id=self.device((self.me + k) % self.parts),
                device_id_type=MESH,
            )
            copy.start()
            self.copies.append(copy)

    def finish(self, src):
        for copy in self.copies:
            copy.wait()

        @pl.when(self.me == 0)
        def _():
            for k in range(1, self.parts):
                self.copy(k, src).wait_send()


def spread_sems(parts):
    dma = pltpu.SemaphoreType.DMA
    return [dma((parts,)), dma, dma((parts,)), dma((parts,))]


def spread_kernel(nr, nc, xr, xc, t, pr, pc, ts, *sems):
    rows_sems, cols_sems, (send, recv, down_send, down_recv) = sems[:4], sems[4:8], sems[8:]
    r, c = greet(nr, nc)
    rows = Spread("col", nc, c, r, pr, rows_sems)
    cols = Spread("row", nr, r, c, pc, cols_sems)
    rows.scatter(lambda at: xr.at[at])
    cols.scatter(lambda at: xc.at[at])

    def slice_to(k):
        return pltpu.make_async_remote_copy(
            src_ref=t.at[k], dst_ref=ts, send_sem=send.at[k], recv_sem=recv, device_id=(r, k), device_id_type=MESH
        )

    def down(k):
        return pltpu.make_async_remote_copy(
            src_ref=ts, dst_ref=ts, send_sem=down_send.at[k], recv_sem=down_recv, device_id=(k, c), device_id_type=MESH
        )

    @pl.when((r == 0) & (c == 0))
    def _():
        for k in range(1, nc):
            slice_to(k).start()
        ts[...] = t[0]

    rows.gather(lambda at: xr.at[at])
    cols.gather(lambda at: xc.at[at])

    @pl.when((r == 0) & (c != 0))
    def _():
        slice_to(1).wait_recv()

    @pl.when(r == 0)
    def _():
        for k in range(1, nr):
            down(k).start()

    @pl.when(r != 0)
    def _():
        down(1).wait_recv()

    rows.finish(lambda at: xr.at[at])
    cols.finish(lambda at: xc.at[at])

    @pl.when(r == 0)
    def _():
        for k in range(1, nr):
            down(k).wait_send()

    @pl.when((r == 0) & (c == 0))
    def _():
        for k in range(1, nc):
            slice_to(k).wait_send()


def middle_kernel(
    nr, nc, first, count, gather, a, pr, pc, xc, t, cinv, rinv, f, ft, finv, finvt, out_r, out_c, out_h, er, ec, *rest
):
    out_t, rest = (rest[0], rest[1:]) if gather else (None, rest)
    sr, sc, h, gram, part_r, part_c, part_h, part_g, sum_r, sum_c, sum_h, sum_g, all_g, cols_h, all_h = rest[:15]
    send, recv, *sems = rest[15:]
    b = BAND
    n = a.shape[0]
    size_r, size_c, size_h, size_g = n // nc, n // nr, h.shape[0] // nc, b // nc
    r, c = greet(nr, nc)
    always = r >= 0

    def along(axis, phase, source, target):
        parts, me = (nc, c) if axis == "col" else (nr, r)
        copies = []
        for k in range(1, parts):
            to = (me + k) % parts
            copy = pltpu.make_async_remote_copy(
                src_ref=source(to),
                dst_ref=target(k),
                send_sem=send.at[phase, k],
                recv_sem=recv.at[phase, k],
                device_id=(r, to) if axis == "col" else (to, c),
                device_id_type=MESH,
            )
            copy.start()
            copies.append(copy)
        return copies

    def finish(copies):
        for copy in copies:
            copy.wait()

    def block(body):
        pl.when(always)(body)

    @block
    def _():
        gram[...] = mm(pr[...], pr[...], 0, 0)
        part_g[r] = gram[rows_at(c, size_g), :]

    g_copies = along("row", 0, lambda to: gram.at[rows_at(c, size_g)], lambda k: part_g.at[r])
    t_copies = []
    if gather:
        t_copies = along("col", 1, lambda to: t, lambda k: out_t.at[c])
        out_t[c] = t[...]
    rows = Spread("col", nc, c, r, er, sems[:4])
    cols = Spread("row", nr, r, c, ec, sems[4:])
    rows_src = lambda at: a.at[at, first * b : (first + 1) * b]
    cols_src = lambda at: xc.at[at]
    rows.scatter(rows_src)
    cols.scatter(cols_src)

    tile = 2 * b if n % (2 * b) == 0 else b

    @pl.loop(0, n // tile)
    def _(step):
        at = pl.ds(pl.multiple_of(step * tile, tile), tile)
        sr[at, :] = dot(a[at, :], pc[...])

    r_copies = along("col", 2, lambda to: sr.at[rows_at(to, size_r)], lambda k: part_r.at[k])

    finish(g_copies)
    value = part_g[0]
    for k in range(1, nr):
        value = value + part_g[k]
    sum_g[...] = value
    all_g[c] = value
    g_copies = along("col", 3, lambda to: sum_g, lambda k: all_g.at[c])

    @block
    def _():
        h[0:b, :] = mm(pr[...], sr[...], 0, 0)
        h[b : (1 + count) * b, :] = jnp.where(r == 0, sr[first * b : (first + count) * b, :], 0.0)

    h_copies = along("col", 4, lambda to: h.at[rows_at(to, size_h)], lambda k: part_h.at[k])

    @pl.loop(0, n // tile)
    def _(step):
        at = pl.ds(pl.multiple_of(step * tile, tile), tile)
        sc[at, :] = mm(a[:, at], pr[...], 0, 0)

    c_copies = along("row", 5, lambda to: sc.at[rows_at(to, size_c)], lambda k: part_c.at[k])
    rows.gather(rows_src)
    cols.gather(cols_src)
    finish(g_copies)

    @block
    def _():
        invert_chol(whole(all_g), cinv, rinv)

    finish(h_copies)
    value = h[rows_at(c, size_h), :]
    for k in range(1, nc):
        value = value + part_h[k]
    sum_h[...] = value
    cols_h[r] = value
    h_copies = along("row", 6, lambda to: sum_h, lambda k: cols_h.at[r])

    finish(r_copies)
    value = sr[rows_at(c, size_r), :]
    for k in range(1, nc):
        value = value + part_r[k]
    sum_r[...] = value
    out_r[rows_at(c, size_r), :] = value
    r_copies = along("col", 7, lambda to: sum_r, lambda k: out_r.at[rows_at(c, size_r)])

    finish(c_copies)
    value = sc[rows_at(r, size_c), :]
    for k in range(1, nr):
        value = value + part_c[k]
    sum_c[...] = value
    out_c[rows_at(r, size_c), :] = value
    c_copies = along("row", 8, lambda to: sum_c, lambda k: out_c.at[rows_at(r, size_c)])
    finish(t_copies)

    @block
    def _():
        invert_top(piece(out_t, 0) if gather else t[...], rinv, f, ft, finv, finvt)

    finish(h_copies)
    value = cols_h[0]
    for k in range(1, nr):
        value = value + cols_h[k]
    all_h[...] = value
    out_h[rows_at(c, size_h), :] = value
    h_copies = along("col", 9, lambda to: all_h, lambda k: out_h.at[rows_at(c, size_h)])
    for copies in (r_copies, c_copies, h_copies):
        finish(copies)
    rows.finish(rows_src)
    cols.finish(cols_src)


def spread(nr, nc, xr, xc, t):
    dma = pltpu.SemaphoreType.DMA
    return pl.pallas_call(
        functools.partial(spread_kernel, nr, nc),
        out_shape=tuple(jax.ShapeDtypeStruct(s, jnp.float32) for s in (xr.shape, xc.shape, t.shape[1:])),
        in_specs=[pl.BlockSpec(memory_space=VMEM)] * 3,
        out_specs=(pl.BlockSpec(memory_space=VMEM),) * 3,
        scratch_shapes=[*spread_sems(nc), *spread_sems(nr), dma((nc,)), dma, dma((nr,)), dma],
        compiler_params=pltpu.CompilerParams(collective_id=0, has_side_effects=True),
        name="spread",
    )(xr, xc, t)


def middle(nr, nc, first, count, gather, a, pr, pc, xc, t):
    most = max(nr, nc)
    dma = pltpu.SemaphoreType.DMA
    b = BAND
    n = a.shape[0]
    heads = (1 + count) * b
    size_r, size_c, size_h, size_g = n // nc, n // nr, heads // nc, b // nc
    outs = [(b, b)] * 6 + [(n, b), (n, b), (heads, b), (n, b), (n, b)]
    if gather:
        outs.append((nc, *t.shape))
    scratch = [
        (n, b), (n, b), (heads, b), (b, b),
        (nc, size_r, b), (nr, size_c, b), (nc, size_h, b), (nr, size_g, b),
        (size_r, b), (size_c, b), (size_h, b), (size_g, b), (nc, size_g, b), (nr, size_h, b), (size_h, b),
    ]
    return pl.pallas_call(
        functools.partial(middle_kernel, nr, nc, first, count, gather),
        out_shape=tuple(jax.ShapeDtypeStruct(s, jnp.float32) for s in outs),
        in_specs=[pl.BlockSpec(memory_space=VMEM)] * 5,
        out_specs=(pl.BlockSpec(memory_space=VMEM),) * len(outs),
        scratch_shapes=[
            *(VMEM(s, jnp.float32) for s in scratch),
            dma((10, most)), dma((10, most)), *spread_sems(nc), *spread_sems(nr),
        ],
        compiler_params=pltpu.CompilerParams(collective_id=first, has_side_effects=True),
        name=f"middle_{first}",
    )(a, pr, pc, xc, t)


def shards(nr, nc, matrix):
    n = matrix.shape[0]
    b = BAND
    row, col = lax.axis_index("row"), lax.axis_index("col")
    pos = jnp.stack([row, col]).astype(jnp.int32)
    row_ids = row * n + jnp.arange(n, dtype=jnp.int32)
    col_ids = col * n + jnp.arange(n, dtype=jnp.int32)

    where = ((1, 0), (1, 1), (2, 0), (2, 1), (2, 2), (0, 2), (1, 2))
    tops = jnp.stack([matrix[i * b : (i + 1) * b, j * b : (j + 1) * b] for i, j in where])
    tops = tops.reshape(len(where), nc, b // nc, b).transpose(1, 0, 2, 3).reshape(nc, -1, b)
    p1r, p1c, t = spread(
        nr,
        nc,
        jnp.where(row_ids[:, None] >= b, matrix[:, :b], 0.0),
        jnp.where(col_ids[:, None] >= b, matrix[:b].T, 0.0),
        tops,
    )
    *fac, sr, sc, h, er, ec, t = middle(nr, nc, 1, 2, True, matrix, p1r, p1c, matrix[b : 2 * b].T, t)
    one = call(
        step_one_kernel,
        [(n, 2 * b), (n, 2 * b), (n, b), (n, b), (b, b), (b, b)],
        "step_one",
        [VMEM((7, b, b), jnp.float32)],
    )
    left, right, p2r, p2c, t2, a33 = one(pos, *fac, h, h.T, t, p1r, sr, er, p1c, sc, ec)
    updated = matrix - mm(left, right, 1, 1)
    *fac, sr, sc, h, er, ec = middle(nr, nc, 2, 1, False, updated, p2r, p2c, updated[2 * b : 3 * b].T, t2)
    two = call(step_two_kernel, [(n, 2 * b), (n, 2 * b)], "step_two", [VMEM((b, b), jnp.float32)])
    left, right = two(pos, *fac, h, h.T, a33, p2r, sr, er, p2c, sc, ec)
    return updated - mm(left, right, 1, 1)


def solution(mesh):
    spec = P("row", "col")
    body = functools.partial(shards, mesh.shape["row"], mesh.shape["col"])
    return jax.shard_map(body, mesh=mesh, in_specs=(spec,), out_specs=spec, check_vma=False)
```

time: 255 us -> 196 us (0.77)
  Pallas kernels: 211 us -> 165 us
  matrix products: 29.1 us -> 9.21 us
  local copies, waits for them, and re-layouts: 10.4 us -> 17.3 us
    pallas_call x1, Pallas kernels: 57.3 us -> 32.1 us  [spread(): pl.pallas_call(functools.partial(spread_kernel, nr, nc), out_shape=tuple(...]
    dot_general x10 -> x2, matrix products: 29.1 us -> 9.21 us  [mm(): lax.dot_general(left, right, (((ca,), (cb,)), ((), ())), precision=HIGH,...]
    pallas_call x4 -> x2, Pallas kernels: 132 us -> 113 us  [middle(): pl.pallas_call(functools.partial(middle_kernel, nr, nc, first, count, gat...]
    unnamed x19 -> x11, local copies, waits for them, and re-layouts: 2.21 us -> 7.27 us
    sub x0 -> x2, local copies, waits for them, and re-layouts: none -> 4.98 us  [the longest x1 3.04 us: shards(): return updated - mm(left, right, 1, 1)]
where the time goes in v1:
time: 196 us; the launch traced here: 195 us
  Pallas kernels  165 us (84%)
  local copies, waits for them, and re-layouts  17.3 us (9%)
  matrix products  9.21 us (5%)
  other arithmetic  3.7 us (2%)
    pallas_call x2, Pallas kernels, middle(): pl.pallas_call(functools.partial(middle_kernel, nr, nc, first, count, gat...  113 us
    pallas_call x1, Pallas kernels, spread(): pl.pallas_call(functools.partial(spread_kernel, nr, nc), out_shape=tuple(...  32.1 us
    pallas_call x2, Pallas kernels, run(): pl.pallas_call(body, out_shape=tuple((jax.ShapeDtypeStruct(s, jnp.float32...  19.6 us
    dot_general x2, matrix products, mm(): lax.dot_general(left, right, (((ca,), (cb,)), ((), ())), precision=HIGH,...  9.21 us
    unnamed x11, local copies, waits for them, and re-layouts  7.27 us

profile of v1, /device:TPU:1, one launch (start us, length us, event | category | flops | bytes accessed | tf_op | source)
XLA Modules:
  0.0 195.1 jit_solution(60345410775147441)
XLA Ops:
  0.0 0.6 pad_add_fusion.pos_ref
  0.6 1.9 slice_select_fusion.1.xr
  2.5 0.8 bitcast_dynamic-update-slice_fusion.6
  3.4 0.8 bitcast_dynamic-update-slice_fusion.5
  4.2 0.8 bitcast_dynamic-update-slice_fusion.4
  5.1 0.8 bitcast_dynamic-update-slice_fusion.3
  5.9 0.8 bitcast_dynamic-update-slice_fusion.2
  6.8 0.8 bitcast_dynamic-update-slice_fusion.1
  7.6 0.8 bitcast_dynamic-update-slice_fusion
  8.5 0.0 copy-start.1
  8.5 2.2 %copy.12 = f32[768,768]{0,1:T(8,128)S(1)} copy(f32[768,768]{1,0:T(8,128)} %a.1) | data formatting | bytes 4718592 | tf_op args[0]
  10.7 0.0 copy-done.1
  10.7 0.0 copy-start
  10.7 1.2 slice_bitcast_fusion.1
  11.9 32.1 %spread.1 = (f32[768,128]{1,0:T(8,128)}, f32[768,128]{1,0:T(8,128)}, f32[56,128]{1,0:T(8,128)}) custom-call(f32[768,128]{1,0:T(8,128)} %slice_select_fusion.1.xr, f32[768,128]{1,0:T(8,128)} %get-tuple-element.74.xc, f32[16,56,128]{2,1,0:T(8,128)} %bitcast.46), custom_call_target="tpu_custom_call" | custom-call | tf_op jit(solution)/shard_map/spread/pallas_call | solution.py:475
  43.9 58.4 %middle_1.1 = (f32[128,128]{1,0:T(8,128)}, f32[128,128]{1,0:T(8,128)}, f32[128,128]{1,0:T(8,128)}, f32[128,128]{1,0:T(8,128)}, f32[128,128]{1,0:T(8,128)}, /*ind...) custom-call(f32[768,768]{1,0:T(8,128)} %a.1, ...), custom_call_target="tpu_custom_call" | custom-call | tf_op jit(solution)/shard_map/middle_1/pallas_call | solution.py:501
  102.3 0.0 copy-done
  102.3 1.7 copy.11
  104.1 11.8 %step_one.1 = (f32[768,256]{1,0:T(8,128)}, f32[768,256]{1,0:T(8,128)}, f32[768,128]{1,0:T(8,128)}, f32[768,128]{1,0:T(8,128)}, f32[128,128]{1,0:T(8,128)}, /*index=5*/f32[128,128]{1,0:T(8,128)}) custom-call(s32[2]{0:T(128)} %pad_add_fusion.pos_ref, f32[128,128]{1,0:T(8,128)} %get-tuple-element.42.cinv_ref, f32[128,128]{1,0:T(8,128)} %get-tuple-element.43.rinv_ref, ...), custom_call_target="tpu_custom_call" | custom-call | tf_op jit(solution)/shard_map/step_one/pallas_call | solution.py:197
  115.9 4.3 %convolution_subtract_fusion.1 = f32[768,768]{0,1:T(8,128)S(1)} fusion(f32[768,768]{0,1:T(8,128)} %copy-done, f32[768,256]{1,0:T(8,128)} %get-tuple-element.54, f32[768,256]{1,0:T(8,128)} %get-tuple-element.55), kind=kOutput, calls=%fused_computation.1 | convolution fusion | flops 1812529152 | bytes 6291456 | tf_op jit(solution)/shard_map/dot_general | solution.py:21
  120.2 0.8 slice_bitcast_fusion.xc
  120.9 1.9 copy.14.a
  122.9 54.7 %middle_2.1 = (f32[128,128]{1,0:T(8,128)}, f32[128,128]{1,0:T(8,128)}, f32[128,128]{1,0:T(8,128)}, f32[128,128]{1,0:T(8,128)}, f32[128,128]{1,0:T(8,128)}, /*ind...) custom-call(f32[768,768]{1,0:T(8,128)} %copy.14.a, ...), custom_call_target="tpu_custom_call" | custom-call | tf_op jit(solution)/shard_map/middle_2/pallas_call | solution.py:501
  177.6 1.7 copy.15
  179.3 7.9 %step_two.1 = (f32[768,256]{1,0:T(8,128)}, f32[768,256]{1,0:T(8,128)}) custom-call(s32[2]{0:T(128)} %pad_add_fusion.pos_ref, f32[128,128]{1,0:T(8,128)} %get-tuple-element.59.cinv_ref, f32[128,128]{1,0:T(8,128)} %get-tuple-element.60.rinv_ref, f32[128,128]{1,0:T(8,128)} %get-tuple-element.61.f_ref, f32[128,128]{1,0:T(8,128)} %get-tuple-element.62.ft_ref, ...), custom_call_target="tpu_custom_call" | custom-call | tf_op jit(solution)/shard_map/step_two/pallas_call | solution.py:197
  187.1 4.9 %convolution_subtract_fusion = f32[768,768]{0,1:T(8,128)} fusion(f32[768,768]{0,1:T(8,128)S(1)} %convolution_subtract_fusion.1, f32[768,256]{1,0:T(8,128)} %get-tuple-element.71, f32[768,256]{1,0:T(8,128)} %get-tuple-element.72), kind=kOutput, calls=%fused_computation | convolution fusion | flops 1812529152 | bytes 6291456 | tf_op jit(solution)/shard_map/dot_general | solution.py:21
  192.0 3.0 %copy.17 = f32[768,768]{1,0:T(8,128)} copy(f32[768,768]{0,1:T(8,128)} %convolution_subtract_fusion) | data formatting | bytes 4718592 | tf_op jit(solution)/shard_map/sub | solution.py:545
  (2 shorter events, 0.0 us)
Async XLA Ops:
  8.5 2.2 %copy-start.1 = (f32[7,16,8,128]{3,2,0,1:T(8,128)}, f32[7,16,8,128]{3,2,0,1:T(8,128)S(1)}, u32[]{:S(2)}) copy-start(f32[7,16,8,128]{3,2,0,1:T(8,128)S(1)} %bitcast_dynamic-update-slice_fusion) | copy-start | bytes 1376260
  10.7 91.6 %copy-start = (f32[768,768]{0,1:T(8,128)}, f32[768,768]{0,1:T(8,128)S(1)}, u32[]{:S(2)}) copy-start(f32[768,768]{0,1:T(8,128)S(1)} %copy.12) | copy-start | bytes 7077892

commit v2 on v1

--- a/solution.py
+++ b/solution.py
@@ -27,30 +27,34 @@
     n = x_ref.shape[0]
     lane = lax.broadcasted_iota(jnp.int32, (1, n), 1)
     rows = lax.broadcasted_iota(jnp.int32, (n, 1), 0)
-    rows8 = lax.broadcasted_iota(jnp.int32, (8, 1), 0)
+    rows8 = lax.broadcasted_iota(jnp.int32, (8, n), 0)
+    lane8 = lax.broadcasted_iota(jnp.int32, (8, n), 1)
 
     def block(j, _):
+        at = pl.ds(pl.multiple_of(8 * j, 8), 8)
         full = x_ref[...]
-        strip = x_ref[pl.ds(pl.multiple_of(8 * j, 8), 8), :]
+        strip = x_ref[at, :]
+        cols = [jnp.broadcast_to(strip[:, i : i + 1], (8, n)) for i in range(8)]
+        kept = strip
         for i in range(8):
-            row = strip[i : i + 1, :]
-            inv = 1.0 / row[:, i : i + 1]
-            here = lane == i
-            row = jnp.where(here, 1.0, row)
-
-            def update(x, ids):
-                col = x[:, i : i + 1] * inv
-                if jordan:
-                    pivot = ids == i
-                    col = jnp.where(pivot, -inv, col)
-                    return jnp.where(here | pivot, 0.0, x) - col * row
-                below = ids > i
-                col = jnp.where(below, col, 0.0)
-                return jnp.where(here & below, 0.0, x) - col * row
-
-            full = update(full, rows - 8 * j)
-            strip = update(strip, rows8)
-        x_ref[...] = pltpu.roll(full, n - 8, 1)
+            if not jordan:
+                kept = jnp.where(rows8 == i, strip, kept)
+            inv = 1.0 / jnp.broadcast_to(cols[i][i : i + 1, :], (8, n))
+            mult = jnp.where(rows8 == i, -inv, cols[i] * inv)
+            for k in range(i + 1, 8):
+                cols[k] = jnp.where(rows8 == i, 0.0, cols[k]) - mult * cols[k][i : i + 1, :]
+            row = jnp.where(lane == i, 1.0, strip[i : i + 1, :])
+            strip = jnp.where((rows8 == i) | (lane8 == i), 0.0, strip) - mult * row
+        ids = rows - 8 * j
+        out = jnp.where(lane < 8, 0.0, full)
+        for i in range(8):
+            out = out - full[:, i : i + 1] * strip[i : i + 1, :]
+        if jordan:
+            x_ref[...] = pltpu.roll(out, n - 8, 1)
+            x_ref[at, :] = pltpu.roll(strip, n - 8, 1)
+        else:
+            x_ref[...] = pltpu.roll(jnp.where(ids >= 8, out, full), n - 8, 1)
+            x_ref[at, :] = pltpu.roll(kept, n - 8, 1)
         return 0
 
     lax.fori_loop(0, n // 8, block, 0)
@@ -100,15 +104,21 @@
 
 
 def step_one_kernel(
-    pos_ref, cinv_ref, rinv_ref, f_ref, ft_ref, finv_ref, finvt_ref, h_ref, ht_ref, g_ref,
-    pr_ref, sr_ref, er_ref, pc_ref, sc_ref, ec_ref,
-    left_ref, right_ref, p2r_ref, p2c_ref, t2_ref, a33_ref, small_ref,
+    pos_ref, cinv_ref, rinv_ref, f_ref, ft_ref, finv_ref, finvt_ref, h_ref, g_ref,
+    pr_ref, sr_ref, er_ref, pc_ref, sc_ref, ec_ref, a_ref,
+    updated_ref, p2r_ref, p2c_ref, t2_ref, a33_ref, left_ref, right_ref, ht_ref, small_ref,
 ):
     b = BAND
     n = pr_ref.shape[0]
     always = pos_ref[0] >= 0
     sums = lambda k: h_ref[k * b : (k + 1) * b, :]
     sumst = lambda k: ht_ref[:, k * b : (k + 1) * b]
+
+    @pl.when(always)
+    def _():
+        for k in range(3):
+            ht_ref[:, k * b : (k + 1) * b] = h_ref[k * b : (k + 1) * b, :].T
+
     a22, a31, a32, a33, a13, a23 = (functools.partial(piece, g_ref, k) for k in range(1, 7))
 
     @pl.when(always)
@@ -162,11 +172,16 @@
     side(pos_ref[0], pr_ref, sr_ref, er_ref, left_ref, 0, b, p2r_ref)
     side(pos_ref[1], pc_ref, sc_ref, ec_ref, right_ref, b, 0, p2c_ref)
 
+    @pl.loop(0, n // tile)
+    def _(step):
+        at = pl.ds(pl.multiple_of(step * tile, tile), tile)
+        updated_ref[at, :] = a_ref[at, :] - mm(left_ref[at, :], right_ref[...], 1, 1)
+
 
 def step_two_kernel(
-    pos_ref, cinv_ref, rinv_ref, f_ref, ft_ref, finv_ref, finvt_ref, h_ref, ht_ref, a33_ref,
-    pr_ref, sr_ref, er_ref, pc_ref, sc_ref, ec_ref,
-    left_ref, right_ref, z_ref,
+    pos_ref, cinv_ref, rinv_ref, f_ref, ft_ref, finv_ref, finvt_ref, h_ref, a33_ref,
+    pr_ref, sr_ref, er_ref, pc_ref, sc_ref, ec_ref, a_ref,
+    out_ref, left_ref, right_ref, ht_ref, z_ref, result_ref, sem,
 ):
     b = BAND
     n = pr_ref.shape[0]
@@ -174,8 +189,12 @@
 
     @pl.when(pos_ref[0] >= 0)
     def _():
+        ht_ref[...] = h_ref[b : 2 * b, :].T
+
+    @pl.when(pos_ref[0] >= 0)
+    def _():
         fac = tuple(ref[...] for ref in (cinv_ref, rinv_ref, f_ref, ft_ref, finv_ref, finvt_ref))
-        z_ref[...] = weights(fac, h_ref[0:b, :], h_ref[b : 2 * b, :], ht_ref[:, b : 2 * b], a33_ref[...])
+        z_ref[...] = weights(fac, h_ref[0:b, :], h_ref[b : 2 * b, :], ht_ref[...], a33_ref[...])
 
     def side(start, p_ref, s_ref, e_ref, out_ref, house_at, work_at):
         @pl.loop(0, n // tile)
@@ -191,14 +210,28 @@
     side(pos_ref[0], pr_ref, sr_ref, er_ref, left_ref, 0, b)
     side(pos_ref[1], pc_ref, sc_ref, ec_ref, right_ref, b, 0)
 
-
-def call(body, outs, name, scratch=()):
+    def store(step):
+        at = pl.ds(pl.multiple_of(step * tile, tile), tile)
+        return pltpu.make_async_copy(result_ref.at[at], out_ref.at[at], sem.at[step])
+
+    @pl.loop(0, n // tile)
+    def _(step):
+        at = pl.ds(pl.multiple_of(step * tile, tile), tile)
+        result_ref[at, :] = a_ref[at, :] - mm(left_ref[at, :], right_ref[...], 1, 1)
+        store(step).start()
+
+    @pl.loop(0, n // tile)
+    def _(step):
+        store(step).wait()
+
+
+def call(body, outs, name, scratch, space=VMEM):
     def run(pos, *args):
         return pl.pallas_call(
             body,
             out_shape=tuple(jax.ShapeDtypeStruct(s, jnp.float32) for s in outs),
             in_specs=[pl.BlockSpec(memory_space=pltpu.SMEM)] + [pl.BlockSpec(memory_space=VMEM)] * len(args),
-            out_specs=(pl.BlockSpec(memory_space=VMEM),) * len(outs),
+            out_specs=(pl.BlockSpec(memory_space=space),) * len(outs),
             scratch_shapes=scratch,
             name=name,
         )(pos, *args)
@@ -206,15 +239,23 @@
     return run
 
 
-def greet(nr, nc):
+def greet(nr, nc, between=None):
     r, c = lax.axis_index("row"), lax.axis_index("col")
     barrier = pltpu.get_barrier_semaphore()
     for k in range(1, nc):
         pl.semaphore_signal(barrier, inc=1, device_id=(r, (c + k) % nc), device_id_type=MESH)
     for k in range(1, nr):
         pl.semaphore_signal(barrier, inc=1, device_id=((r + k) % nr, c), device_id_type=MESH)
+    if between is not None:
+        between(r, c)
     pl.semaphore_wait(barrier, nr + nc - 2)
     return r, c
+
+
+def turn(a, block, out):
+    for k in range(a.shape[1] // BAND):
+        at = pl.ds(k * BAND, BAND)
+        out[at, :] = a[pl.ds(block * BAND, BAND), at].T
 
 
 def rows_at(index, size):
@@ -283,9 +324,29 @@
     return [dma((parts,)), dma, dma((parts,)), dma((parts,))]
 
 
-def spread_kernel(nr, nc, xr, xc, t, pr, pc, ts, *sems):
+def spread_kernel(nr, nc, a, pr, pc, ts, xr, xc, t, *sems):
     rows_sems, cols_sems, (send, recv, down_send, down_recv) = sems[:4], sems[4:8], sems[8:]
-    r, c = greet(nr, nc)
+    b = BAND
+
+    def prepare(r, c):
+        @pl.when(c == 0)
+        def _():
+            xr[...] = a[:, 0:b]
+
+        @pl.when(r == 0)
+        def _():
+            turn(a, 0, xc)
+
+        @pl.when((r == 0) & (c == 0))
+        def _():
+            xr[0:b, :] = jnp.zeros((b, b), jnp.float32)
+            xc[0:b, :] = jnp.zeros((b, b), jnp.float32)
+            rows = b // nc
+            for k, (i, j) in enumerate(((1, 0), (1, 1), (2, 0), (2, 1), (2, 2), (0, 2), (1, 2))):
+                block = a[i * b : (i + 1) * b, j * b : (j + 1) * b]
+                t[:, k * rows : (k + 1) * rows, :] = block.reshape(nc, rows, b)
+
+    r, c = greet(nr, nc, prepare)
     rows = Spread("col", nc, c, r, pr, rows_sems)
     cols = Spread("row", nr, r, c, pc, cols_sems)
     rows.scatter(lambda at: xr.at[at])
@@ -338,15 +399,26 @@
 
 
 def middle_kernel(
-    nr, nc, first, count, gather, a, pr, pc, xc, t, cinv, rinv, f, ft, finv, finvt, out_r, out_c, out_h, er, ec, *rest
+    nr, nc, first, count, gather, a, pr, pc, t, cinv, rinv, f, ft, finv, finvt, out_r, out_c, out_h, er, ec, *rest
 ):
     out_t, rest = (rest[0], rest[1:]) if gather else (None, rest)
-    sr, sc, h, gram, part_r, part_c, part_h, part_g, sum_r, sum_c, sum_h, sum_g, all_g, cols_h, all_h = rest[:15]
-    send, recv, *sems = rest[15:]
+    sr, sc, h, gram, part_r, part_c, part_h, part_g, sum_r, sum_c, sum_h, sum_g, all_g, cols_h, all_h, xc = rest[:16]
+    send, recv, *sems = rest[16:]
     b = BAND
     n = a.shape[0]
     size_r, size_c, size_h, size_g = n // nc, n // nr, h.shape[0] // nc, b // nc
-    r, c = greet(nr, nc)
+
+    def prepare(r, c):
+        @pl.when(r >= 0)
+        def _():
+            gram[...] = mm(pr[...], pr[...], 0, 0)
+            part_g[r] = gram[rows_at(c, size_g), :]
+
+        @pl.when(r == 0)
+        def _():
+            turn(a, first, xc)
+
+    r, c = greet(nr, nc, prepare)
     always = r >= 0
 
     def along(axis, phase, source, target):
@@ -373,11 +445,6 @@
     def block(body):
         pl.when(always)(body)
 
-    @block
-    def _():
-        gram[...] = mm(pr[...], pr[...], 0, 0)
-        part_g[r] = gram[rows_at(c, size_g), :]
-
     g_copies = along("row", 0, lambda to: gram.at[rows_at(c, size_g)], lambda k: part_g.at[r])
     t_copies = []
     if gather:
@@ -470,20 +537,26 @@
     cols.finish(cols_src)
 
 
-def spread(nr, nc, xr, xc, t):
+def spread(nr, nc, a):
     dma = pltpu.SemaphoreType.DMA
+    b = BAND
+    n = a.shape[0]
+    tops = 7 * b // nc
     return pl.pallas_call(
         functools.partial(spread_kernel, nr, nc),
-        out_shape=tuple(jax.ShapeDtypeStruct(s, jnp.float32) for s in (xr.shape, xc.shape, t.shape[1:])),
-        in_specs=[pl.BlockSpec(memory_space=VMEM)] * 3,
+        out_shape=tuple(jax.ShapeDtypeStruct(s, jnp.float32) for s in ((n, b), (n, b), (tops, b))),
+        in_specs=[pl.BlockSpec(memory_space=VMEM)],
         out_specs=(pl.BlockSpec(memory_space=VMEM),) * 3,
-        scratch_shapes=[*spread_sems(nc), *spread_sems(nr), dma((nc,)), dma, dma((nr,)), dma],
+        scratch_shapes=[
+            *(VMEM(s, jnp.float32) for s in ((n, b), (n, b), (nc, tops, b))),
+            *spread_sems(nc), *spread_sems(nr), dma((nc,)), dma, dma((nr,)), dma,
+        ],
         compiler_params=pltpu.CompilerParams(collective_id=0, has_side_effects=True),
         name="spread",
-    )(xr, xc, t)
-
-
-def middle(nr, nc, first, count, gather, a, pr, pc, xc, t):
+    )(a)
+
+
+def middle(nr, nc, first, count, gather, a, pr, pc, t):
     most = max(nr, nc)
     dma = pltpu.SemaphoreType.DMA
     b = BAND
@@ -496,12 +569,12 @@
     scratch = [
         (n, b), (n, b), (heads, b), (b, b),
         (nc, size_r, b), (nr, size_c, b), (nc, size_h, b), (nr, size_g, b),
-        (size_r, b), (size_c, b), (size_h, b), (size_g, b), (nc, size_g, b), (nr, size_h, b), (size_h, b),
+        (size_r, b), (size_c, b), (size_h, b), (size_g, b), (nc, size_g, b), (nr, size_h, b), (size_h, b), (n, b),
     ]
     return pl.pallas_call(
         functools.partial(middle_kernel, nr, nc, first, count, gather),
         out_shape=tuple(jax.ShapeDtypeStruct(s, jnp.float32) for s in outs),
-        in_specs=[pl.BlockSpec(memory_space=VMEM)] * 5,
+        in_specs=[pl.BlockSpec(memory_space=VMEM)] * 4,
         out_specs=(pl.BlockSpec(memory_space=VMEM),) * len(outs),
         scratch_shapes=[
             *(VMEM(s, jnp.float32) for s in scratch),
@@ -509,7 +582,7 @@
         ],
         compiler_params=pltpu.CompilerParams(collective_id=first, has_side_effects=True),
         name=f"middle_{first}",
-    )(a, pr, pc, xc, t)
+    )(a, pr, pc, t)
 
 
 def shards(nr, nc, matrix):
@@ -517,32 +590,25 @@
     b = BAND
     row, col = lax.axis_index("row"), lax.axis_index("col")
     pos = jnp.stack([row, col]).astype(jnp.int32)
-    row_ids = row * n + jnp.arange(n, dtype=jnp.int32)
-    col_ids = col * n + jnp.arange(n, dtype=jnp.int32)
-
-    where = ((1, 0), (1, 1), (2, 0), (2, 1), (2, 2), (0, 2), (1, 2))
-    tops = jnp.stack([matrix[i * b : (i + 1) * b, j * b : (j + 1) * b] for i, j in where])
-    tops = tops.reshape(len(where), nc, b // nc, b).transpose(1, 0, 2, 3).reshape(nc, -1, b)
-    p1r, p1c, t = spread(
-        nr,
-        nc,
-        jnp.where(row_ids[:, None] >= b, matrix[:, :b], 0.0),
-        jnp.where(col_ids[:, None] >= b, matrix[:b].T, 0.0),
-        tops,
-    )
-    *fac, sr, sc, h, er, ec, t = middle(nr, nc, 1, 2, True, matrix, p1r, p1c, matrix[b : 2 * b].T, t)
+    vmem = lambda *shape: VMEM(shape, jnp.float32)
+    p1r, p1c, t = spread(nr, nc, matrix)
+    *fac, sr, sc, h, er, ec, t = middle(nr, nc, 1, 2, True, matrix, p1r, p1c, t)
     one = call(
         step_one_kernel,
-        [(n, 2 * b), (n, 2 * b), (n, b), (n, b), (b, b), (b, b)],
+        [(n, n), (n, b), (n, b), (b, b), (b, b)],
         "step_one",
-        [VMEM((7, b, b), jnp.float32)],
+        [vmem(n, 2 * b), vmem(n, 2 * b), vmem(b, 3 * b), vmem(7, b, b)],
     )
-    left, right, p2r, p2c, t2, a33 = one(pos, *fac, h, h.T, t, p1r, sr, er, p1c, sc, ec)
-    updated = matrix - mm(left, right, 1, 1)
-    *fac, sr, sc, h, er, ec = middle(nr, nc, 2, 1, False, updated, p2r, p2c, updated[2 * b : 3 * b].T, t2)
-    two = call(step_two_kernel, [(n, 2 * b), (n, 2 * b)], "step_two", [VMEM((b, b), jnp.float32)])
-    left, right = two(pos, *fac, h, h.T, a33, p2r, sr, er, p2c, sc, ec)
-    return updated - mm(left, right, 1, 1)
+    updated, p2r, p2c, t2, a33 = one(pos, *fac, h, t, p1r, sr, er, p1c, sc, ec, matrix)
+    *fac, sr, sc, h, er, ec = middle(nr, nc, 2, 1, False, updated, p2r, p2c, t2)
+    two = call(
+        step_two_kernel,
+        [(n, n)],
+        "step_two",
+        [vmem(n, 2 * b), vmem(n, 2 * b), vmem(b, b), vmem(b, b), vmem(n, n), pltpu.SemaphoreType.DMA((n // b,))],
+        pl.ANY,
+    )
+    return two(pos, *fac, h, a33, p2r, sr, er, p2c, sc, ec, updated)[0]
 
 
 def solution(mesh):

time: 196 us -> 164 us (0.84)
  local copies, waits for them, and re-layouts: 17.3 us -> 0 us
  matrix products: 9.21 us -> 0 us
  other arithmetic: 3.7 us -> 0.66 us
  Pallas kernels: 165 us -> 163 us
    dot_general x2 -> x0, matrix products: 9.21 us -> none  [mm(): lax.dot_general(left, right, (((ca,), (cb,)), ((), ())), precision=HIGH,...]
    pallas_call x2, Pallas kernels: 113 us -> 104 us  [middle(): pl.pallas_call(functools.partial(middle_kernel, nr, nc, first, count, gat...]
    unnamed x11 -> x0, local copies, waits for them, and re-layouts: 7.27 us -> none
    pallas_call x2, Pallas kernels: 19.6 us -> 26.5 us  [run(): pl.pallas_call(body, out_shape=tuple((jax.ShapeDtypeStruct(s, jnp.float32...]
    sub x2 -> x0, local copies, waits for them, and re-layouts: 4.98 us -> none  [the longest x1 3.04 us: shards(): return updated - mm(left, right, 1, 1)]
    pallas_call x2 -> x0, local copies, waits for them, and re-layouts: 3.4 us -> none  [middle(): pl.pallas_call(functools.partial(middle_kernel, nr, nc, first, count, gat...]
where the time goes in v2:
time: 164 us
  Pallas kernels  163 us (99%)
    pallas_call x2, Pallas kernels, middle(): pl.pallas_call(functools.partial(middle_kernel, nr, nc, first, count, gat...  104 us
    pallas_call x1, Pallas kernels, spread(): pl.pallas_call(functools.partial(spread_kernel, nr, nc), out_shape=tuple(...  32.5 us
    pallas_call x2, Pallas kernels, run(): pl.pallas_call(body, out_shape=tuple((jax.ShapeDtypeStruct(s, jnp.float32...  26.5 us

profile of v2, /device:TPU:1, one launch (start us, length us, event | category | flops | bytes accessed | tf_op | source)
XLA Modules:
  0.0 164.0 jit_solution(14632802092814267067)
XLA Ops:
  0.0 0.7 pad_add_fusion.pos_ref
  0.7 32.5 %spread.1 = (f32[768,128]{1,0:T(8,128)}, f32[768,128]{1,0:T(8,128)}, f32[56,128]{1,0:T(8,128)}) custom-call(f32[768,768]{1,0:T(8,128)} %a_ref.1), custom_call_target="tpu_custom_call" | custom-call | tf_op jit(solution)/shard_map/spread/pallas_call | solution.py:545
  33.1 53.1 %middle_1.1 = (f32[128,128]{1,0:T(8,128)}, f32[128,128]{1,0:T(8,128)}, f32[128,128]{1,0:T(8,128)}, f32[128,128]{1,0:T(8,128)}, f32[128,128]{1,0:T(8,128)}, /*ind...) custom-call(f32[768,768]{1,0:T(8,128)} %a_ref.1, ...), custom_call_target="tpu_custom_call" | custom-call | tf_op jit(solution)/shard_map/middle_1/pallas_call | solution.py:574
  86.2 15.5 %step_one.1 = (f32[768,768]{1,0:T(8,128)}, f32[768,128]{1,0:T(8,128)}, f32[768,128]{1,0:T(8,128)}, f32[128,128]{1,0:T(8,128)}, f32[128,128]{1,0:T(8,128)}) custom-call(s32[2]{0:T(128)} %pad_add_fusion.pos_ref, f32[128,128]{1,0:T(8,128)} %get-tuple-element.39.cinv_ref, f32[128,128]{1,0:T(8,128)} %get-tuple-element.40.rinv_ref, ...), custom_call_target="tpu_custom_call" | custom-call | tf_op jit(solution)/shard_map/step_one/pallas_call | solution.py:230
  101.7 51.2 %middle_2.1 = (f32[128,128]{1,0:T(8,128)}, f32[128,128]{1,0:T(8,128)}, f32[128,128]{1,0:T(8,128)}, f32[128,128]{1,0:T(8,128)}, f32[128,128]{1,0:T(8,128)}, /*ind...) custom-call(f32[768,768]{1,0:T(8,128)} %get-tuple-element.51.a.a_ref, ...), custom_call_target="tpu_custom_call" | custom-call | tf_op jit(solution)/shard_map/middle_2/pallas_call | solution.py:574
  152.9 11.0 %step_two.1 = f32[768,768]{1,0:T(8,128)} custom-call(s32[2]{0:T(128)} %pad_add_fusion.pos_ref, f32[128,128]{1,0:T(8,128)} %get-tuple-element.55.cinv_ref, f32[128,128]{1,0:T(8,128)} %get-tuple-element.56.rinv_ref, f32[128,128]{1,0:T(8,128)} %get-tuple-element.57.f_ref, f32[128,128]{1,0:T(8,128)} %get-tuple-element.58.ft_ref, ...), custom_call_target="tpu_custom_call" | custom-call | tf_op jit(solution)/shard_map/step_two/pallas_call | solution.py:230

commit v3 on v2

--- a/solution.py
+++ b/solution.py
@@ -263,7 +263,8 @@
 
 
 class Spread:
-    def __init__(self, axis, parts, me, other, dst, sems):
+    def __init__(self, axis, parts, me, other, dst, sems, pair_sems=None):
+        self.pair = None if pair_sems is None else PairGather(me, other, parts, dst, pair_sems)
         self.axis, self.parts, self.me, self.other, self.dst = axis, parts, me, other, dst
         self.root_send, self.root_recv, self.send, self.recv = sems
         self.size = dst.shape[0] // parts
@@ -296,6 +297,9 @@
             self.copy(1, src).wait_recv()
 
         self.copies = []
+        if self.pair is not None:
+            self.pair.start()
+            return
         for k in range(1, self.parts):
             rows = rows_at(self.me, self.size)
             copy = pltpu.make_async_remote_copy(
@@ -312,11 +316,61 @@
     def finish(self, src):
         for copy in self.copies:
             copy.wait()
+        if self.pair is not None:
+            self.pair.finish()
 
         @pl.when(self.me == 0)
         def _():
             for k in range(1, self.parts):
                 self.copy(k, src).wait_send()
+
+
+class PairGather:
+    def __init__(self, r, c, nr, dst, sems):
+        self.r, self.c, self.count, self.dst = r, c, nr // 2, dst
+        self.z, self.p = r // 2, r % 2
+        self.sems = sems
+        self.size = dst.shape[0] // nr
+
+    def copy(self, src, index, to, stage, k):
+        return pltpu.make_async_remote_copy(
+            src_ref=src,
+            dst_ref=self.dst.at[rows_at(index, self.size)],
+            send_sem=self.sems[2 * stage].at[k],
+            recv_sem=self.sems[2 * stage + 1].at[k],
+            device_id=(to, self.c),
+            device_id_type=MESH,
+        )
+
+    def start(self, src=None):
+        src = self.dst.at[rows_at(self.r, self.size)] if src is None else src
+        self.partner = 2 * self.z + 1 - self.p
+        self.far = []
+        for k in range(1, self.count):
+            to = 2 * ((self.z + k) % self.count) + self.p
+            self.far.append(self.copy(src, self.r, to, 0, k))
+        for copy in self.far:
+            copy.start()
+        self.near = [self.copy(src, self.r, self.partner, 1, 0)]
+        self.near[0].start()
+
+    def forward(self):
+        for k in sorted(range(1, self.count), key=lambda k: min(k, self.count - k)):
+            self.far[k - 1].wait_recv()
+            index = 2 * ((self.z + self.count - k) % self.count) + self.p
+            copy = self.copy(self.dst.at[rows_at(index, self.size)], index, self.partner, 1, k)
+            copy.start()
+            self.near.append(copy)
+
+    def finish(self):
+        for copy in self.far:
+            copy.wait_send()
+        for copy in self.near:
+            copy.wait()
+
+
+def pair_sems(nr):
+    return [pltpu.SemaphoreType.DMA((nr // 2,)) for _ in range(4)]
 
 
 def spread_sems(parts):
@@ -325,7 +379,7 @@
 
 
 def spread_kernel(nr, nc, a, pr, pc, ts, xr, xc, t, *sems):
-    rows_sems, cols_sems, (send, recv, down_send, down_recv) = sems[:4], sems[4:8], sems[8:]
+    rows_sems, cols_sems, (send, recv, down_send, down_recv) = sems[:4], sems[4:8], sems[8:12]
     b = BAND
 
     def prepare(r, c):
@@ -348,7 +402,7 @@
 
     r, c = greet(nr, nc, prepare)
     rows = Spread("col", nc, c, r, pr, rows_sems)
-    cols = Spread("row", nr, r, c, pc, cols_sems)
+    cols = Spread("row", nr, r, c, pc, cols_sems, sems[12:])
     rows.scatter(lambda at: xr.at[at])
     cols.scatter(lambda at: xc.at[at])
 
@@ -380,6 +434,8 @@
         for k in range(1, nr):
             down(k).start()
 
+    cols.pair.forward()
+
     @pl.when(r != 0)
     def _():
         down(1).wait_recv()
@@ -402,8 +458,8 @@
     nr, nc, first, count, gather, a, pr, pc, t, cinv, rinv, f, ft, finv, finvt, out_r, out_c, out_h, er, ec, *rest
 ):
     out_t, rest = (rest[0], rest[1:]) if gather else (None, rest)
-    sr, sc, h, gram, part_r, part_c, part_h, part_g, sum_r, sum_c, sum_h, sum_g, all_g, cols_h, all_h, xc = rest[:16]
-    send, recv, *sems = rest[16:]
+    sr, sc, h, gram, part_r, part_c, part_h, part_g, sum_r, sum_c, sum_h, sum_g, all_g, cols_h, all_h, xc, part_p, sum_p = rest[:18]
+    send, recv, *sems = rest[18:]
     b = BAND
     n = a.shape[0]
     size_r, size_c, size_h, size_g = n // nc, n // nr, h.shape[0] // nc, b // nc
@@ -451,7 +507,8 @@
         t_copies = along("col", 1, lambda to: t, lambda k: out_t.at[c])
         out_t[c] = t[...]
     rows = Spread("col", nc, c, r, er, sems[:4])
-    cols = Spread("row", nr, r, c, ec, sems[4:])
+    cols = Spread("row", nr, r, c, ec, sems[4:8], sems[8:12])
+    gather_c = PairGather(r, c, nr, out_c, sems[12:])
     rows_src = lambda at: a.at[at, first * b : (first + 1) * b]
     cols_src = lambda at: xc.at[at]
     rows.scatter(rows_src)
@@ -474,19 +531,48 @@
     all_g[c] = value
     g_copies = along("col", 3, lambda to: sum_g, lambda k: all_g.at[c])
 
-    @block
-    def _():
-        h[0:b, :] = mm(pr[...], sr[...], 0, 0)
-        h[b : (1 + count) * b, :] = jnp.where(r == 0, sr[first * b : (first + count) * b, :], 0.0)
-
-    h_copies = along("col", 4, lambda to: h.at[rows_at(to, size_h)], lambda k: part_h.at[k])
-
     @pl.loop(0, n // tile)
     def _(step):
         at = pl.ds(pl.multiple_of(step * tile, tile), tile)
         sc[at, :] = mm(a[:, at], pr[...], 0, 0)
 
-    c_copies = along("row", 5, lambda to: sc.at[rows_at(to, size_c)], lambda k: part_c.at[k])
+    z, p = r // 2, r % 2
+    half = nr // 2
+    p_copies = []
+    for i in range(half):
+        copy = pltpu.make_async_remote_copy(
+            src_ref=sc.at[rows_at(2 * i + 1 - p, size_c)],
+            dst_ref=part_p.at[i],
+            send_sem=send.at[5, i],
+            recv_sem=recv.at[5, i],
+            device_id=(2 * z + 1 - p, c),
+            device_id_type=MESH,
+        )
+        copy.start()
+        p_copies.append(copy)
+
+    @block
+    def _():
+        h[0:b, :] = mm(pr[...], sr[...], 0, 0)
+        h[b : (1 + count) * b, :] = jnp.where(r == 0, sr[first * b : (first + count) * b, :], 0.0)
+
+    h_copies = along("col", 4, lambda to: h.at[rows_at(to, size_h)], lambda k: part_h.at[k])
+    finish(p_copies)
+    for i in range(half):
+        sum_p[i] = sc[rows_at(2 * i + p, size_c), :] + part_p[i]
+    c_copies = []
+    for k in range(1, half):
+        to = (z + k) % half
+        copy = pltpu.make_async_remote_copy(
+            src_ref=sum_p.at[to],
+            dst_ref=part_c.at[k],
+            send_sem=send.at[8, k],
+            recv_sem=recv.at[8, k],
+            device_id=(2 * to + p, c),
+            device_id_type=MESH,
+        )
+        copy.start()
+        c_copies.append(copy)
     rows.gather(rows_src)
     cols.gather(cols_src)
     finish(g_copies)
@@ -512,12 +598,12 @@
     r_copies = along("col", 7, lambda to: sum_r, lambda k: out_r.at[rows_at(c, size_r)])
 
     finish(c_copies)
-    value = sc[rows_at(r, size_c), :]
-    for k in range(1, nr):
+    value = sum_p[z]
+    for k in range(1, half):
         value = value + part_c[k]
     sum_c[...] = value
     out_c[rows_at(r, size_c), :] = value
-    c_copies = along("row", 8, lambda to: sum_c, lambda k: out_c.at[rows_at(r, size_c)])
+    gather_c.start(sum_c)
     finish(t_copies)
 
     @block
@@ -531,8 +617,11 @@
     all_h[...] = value
     out_h[rows_at(c, size_h), :] = value
     h_copies = along("col", 9, lambda to: all_h, lambda k: out_h.at[rows_at(c, size_h)])
-    for copies in (r_copies, c_copies, h_copies):
+    gather_c.forward()
+    cols.pair.forward()
+    for copies in (r_copies, h_copies):
         finish(copies)
+    gather_c.finish()
     rows.finish(rows_src)
     cols.finish(cols_src)
 
@@ -549,7 +638,7 @@
         out_specs=(pl.BlockSpec(memory_space=VMEM),) * 3,
         scratch_shapes=[
             *(VMEM(s, jnp.float32) for s in ((n, b), (n, b), (nc, tops, b))),
-            *spread_sems(nc), *spread_sems(nr), dma((nc,)), dma, dma((nr,)), dma,
+            *spread_sems(nc), *spread_sems(nr), dma((nc,)), dma, dma((nr,)), dma, *pair_sems(nr),
         ],
         compiler_params=pltpu.CompilerParams(collective_id=0, has_side_effects=True),
         name="spread",
@@ -568,8 +657,9 @@
         outs.append((nc, *t.shape))
     scratch = [
         (n, b), (n, b), (heads, b), (b, b),
-        (nc, size_r, b), (nr, size_c, b), (nc, size_h, b), (nr, size_g, b),
+        (nc, size_r, b), (nr // 2, size_c, b), (nc, size_h, b), (nr, size_g, b),
         (size_r, b), (size_c, b), (size_h, b), (size_g, b), (nc, size_g, b), (nr, size_h, b), (size_h, b), (n, b),
+        (nr // 2, size_c, b), (nr // 2, size_c, b),
     ]
     return pl.pallas_call(
         functools.partial(middle_kernel, nr, nc, first, count, gather),
@@ -578,7 +668,8 @@
         out_specs=(pl.BlockSpec(memory_space=VMEM),) * len(outs),
         scratch_shapes=[
             *(VMEM(s, jnp.float32) for s in scratch),
-            dma((10, most)), dma((10, most)), *spread_sems(nc), *spread_sems(nr),
+            dma((10, most)), dma((10, most)),
+            *spread_sems(nc), *spread_sems(nr), *pair_sems(nr), *pair_sems(nr),
         ],
         compiler_params=pltpu.CompilerParams(collective_id=first, has_side_effects=True),
         name=f"middle_{first}",

time: 164 us -> 150 us (0.915)
  Pallas kernels: 163 us -> 149 us
    pallas_call x2, Pallas kernels: 104 us -> 93.8 us  [middle(): pl.pallas_call(functools.partial(middle_kernel, nr, nc, first, count, gat...]
    pallas_call x1, Pallas kernels: 32.5 us -> 29.1 us  [spread(): pl.pallas_call(functools.partial(spread_kernel, nr, nc), out_shape=tuple(...]
where the time goes in v3:
time: 150 us
  Pallas kernels  149 us (99%)
    pallas_call x2, Pallas kernels, middle(): pl.pallas_call(functools.partial(middle_kernel, nr, nc, first, count, gat...  93.8 us
    pallas_call x1, Pallas kernels, spread(): pl.pallas_call(functools.partial(spread_kernel, nr, nc), out_shape=tuple(...  29.1 us
    pallas_call x2, Pallas kernels, run(): pl.pallas_call(body, out_shape=tuple((jax.ShapeDtypeStruct(s, jnp.float32...  26.5 us

profile of v3, /device:TPU:1, one launch (start us, length us, event | category | flops | bytes accessed | tf_op | source)
XLA Modules:
  0.0 150.2 jit_solution(1820733297902251046)
XLA Ops:
  0.0 0.7 pad_add_fusion.pos_ref
  0.7 29.1 %spread.1 = (f32[768,128]{1,0:T(8,128)}, f32[768,128]{1,0:T(8,128)}, f32[56,128]{1,0:T(8,128)}) custom-call(f32[768,768]{1,0:T(8,128)} %a_ref.1), custom_call_target="tpu_custom_call" | custom-call | tf_op jit(solution)/shard_map/spread/pallas_call | solution.py:634
  29.8 51.5 %middle_1.1 = (f32[128,128]{1,0:T(8,128)}, f32[128,128]{1,0:T(8,128)}, f32[128,128]{1,0:T(8,128)}, f32[128,128]{1,0:T(8,128)}, f32[128,128]{1,0:T(8,128)}, /*ind...) custom-call(f32[768,768]{1,0:T(8,128)} %a_ref.1, ...), custom_call_target="tpu_custom_call" | custom-call | tf_op jit(solution)/shard_map/middle_1/pallas_call | solution.py:664
  81.3 15.5 %step_one.1 = (f32[768,768]{1,0:T(8,128)}, f32[768,128]{1,0:T(8,128)}, f32[768,128]{1,0:T(8,128)}, f32[128,128]{1,0:T(8,128)}, f32[128,128]{1,0:T(8,128)}) custom-call(s32[2]{0:T(128)} %pad_add_fusion.pos_ref, f32[128,128]{1,0:T(8,128)} %get-tuple-element.39.cinv_ref, f32[128,128]{1,0:T(8,128)} %get-tuple-element.40.rinv_ref, ...), custom_call_target="tpu_custom_call" | custom-call | tf_op jit(solution)/shard_map/step_one/pallas_call | solution.py:230
  96.8 42.3 %middle_2.1 = (f32[128,128]{1,0:T(8,128)}, f32[128,128]{1,0:T(8,128)}, f32[128,128]{1,0:T(8,128)}, f32[128,128]{1,0:T(8,128)}, f32[128,128]{1,0:T(8,128)}, /*ind...) custom-call(f32[768,768]{1,0:T(8,128)} %get-tuple-element.51.a.a_ref, ...), custom_call_target="tpu_custom_call" | custom-call | tf_op jit(solution)/shard_map/middle_2/pallas_call | solution.py:664
  139.1 11.0 %step_two.1 = f32[768,768]{1,0:T(8,128)} custom-call(s32[2]{0:T(128)} %pad_add_fusion.pos_ref, f32[128,128]{1,0:T(8,128)} %get-tuple-element.55.cinv_ref, f32[128,128]{1,0:T(8,128)} %get-tuple-element.56.rinv_ref, f32[128,128]{1,0:T(8,128)} %get-tuple-element.57.f_ref, f32[128,128]{1,0:T(8,128)} %get-tuple-element.58.ft_ref, ...), custom_call_target="tpu_custom_call" | custom-call | tf_op jit(solution)/shard_map/step_two/pallas_call | solution.py:230

commit v4 on v3

--- a/solution.py
+++ b/solution.py
@@ -502,17 +502,11 @@
         pl.when(always)(body)
 
     g_copies = along("row", 0, lambda to: gram.at[rows_at(c, size_g)], lambda k: part_g.at[r])
-    t_copies = []
-    if gather:
-        t_copies = along("col", 1, lambda to: t, lambda k: out_t.at[c])
-        out_t[c] = t[...]
     rows = Spread("col", nc, c, r, er, sems[:4])
     cols = Spread("row", nr, r, c, ec, sems[4:8], sems[8:12])
     gather_c = PairGather(r, c, nr, out_c, sems[12:])
     rows_src = lambda at: a.at[at, first * b : (first + 1) * b]
     cols_src = lambda at: xc.at[at]
-    rows.scatter(rows_src)
-    cols.scatter(cols_src)
 
     tile = 2 * b if n % (2 * b) == 0 else b
 
@@ -521,7 +515,10 @@
         at = pl.ds(pl.multiple_of(step * tile, tile), tile)
         sr[at, :] = dot(a[at, :], pc[...])
 
-    r_copies = along("col", 2, lambda to: sr.at[rows_at(to, size_r)], lambda k: part_r.at[k])
+    @block
+    def _():
+        h[0:b, :] = mm(pr[...], sr[...], 0, 0)
+        h[b : (1 + count) * b, :] = jnp.where(r == 0, sr[first * b : (first + count) * b, :], 0.0)
 
     finish(g_copies)
     value = part_g[0]
@@ -530,6 +527,12 @@
     sum_g[...] = value
     all_g[c] = value
     g_copies = along("col", 3, lambda to: sum_g, lambda k: all_g.at[c])
+    h_copies = along("col", 4, lambda to: h.at[rows_at(to, size_h)], lambda k: part_h.at[k])
+    r_copies = along("col", 2, lambda to: sr.at[rows_at(to, size_r)], lambda k: part_r.at[k])
+    t_copies = []
+    if gather:
+        t_copies = along("col", 1, lambda to: t, lambda k: out_t.at[c])
+        out_t[c] = t[...]
 
     @pl.loop(0, n // tile)
     def _(step):
@@ -550,13 +553,17 @@
         )
         copy.start()
         p_copies.append(copy)
-
-    @block
-    def _():
-        h[0:b, :] = mm(pr[...], sr[...], 0, 0)
-        h[b : (1 + count) * b, :] = jnp.where(r == 0, sr[first * b : (first + count) * b, :], 0.0)
-
-    h_copies = along("col", 4, lambda to: h.at[rows_at(to, size_h)], lambda k: part_h.at[k])
+    rows.scatter(rows_src)
+    cols.scatter(cols_src)
+
+    finish(h_copies)
+    value = h[rows_at(c, size_h), :]
+    for k in range(1, nc):
+        value = value + part_h[k]
+    sum_h[...] = value
+    cols_h[r] = value
+    h_copies = along("row", 6, lambda to: sum_h, lambda k: cols_h.at[r])
+
     finish(p_copies)
     for i in range(half):
         sum_p[i] = sc[rows_at(2 * i + p, size_c), :] + part_p[i]
@@ -573,21 +580,6 @@
         )
         copy.start()
         c_copies.append(copy)
-    rows.gather(rows_src)
-    cols.gather(cols_src)
-    finish(g_copies)
-
-    @block
-    def _():
-        invert_chol(whole(all_g), cinv, rinv)
-
-    finish(h_copies)
-    value = h[rows_at(c, size_h), :]
-    for k in range(1, nc):
-        value = value + part_h[k]
-    sum_h[...] = value
-    cols_h[r] = value
-    h_copies = along("row", 6, lambda to: sum_h, lambda k: cols_h.at[r])
 
     finish(r_copies)
     value = sr[rows_at(c, size_r), :]
@@ -596,6 +588,19 @@
     sum_r[...] = value
     out_r[rows_at(c, size_r), :] = value
     r_copies = along("col", 7, lambda to: sum_r, lambda k: out_r.at[rows_at(c, size_r)])
+    finish(g_copies)
+
+    @block
+    def _():
+        invert_chol(whole(all_g), cinv, rinv)
+
+    finish(h_copies)
+    value = cols_h[0]
+    for k in range(1, nr):
+        value = value + cols_h[k]
+    all_h[...] = value
+    out_h[rows_at(c, size_h), :] = value
+    h_copies = along("col", 9, lambda to: all_h, lambda k: out_h.at[rows_at(c, size_h)])
 
     finish(c_copies)
     value = sum_p[z]
@@ -604,19 +609,14 @@
     sum_c[...] = value
     out_c[rows_at(r, size_c), :] = value
     gather_c.start(sum_c)
+    rows.gather(rows_src)
+    cols.gather(cols_src)
     finish(t_copies)
 
     @block
     def _():
         invert_top(piece(out_t, 0) if gather else t[...], rinv, f, ft, finv, finvt)
 
-    finish(h_copies)
-    value = cols_h[0]
-    for k in range(1, nr):
-        value = value + cols_h[k]
-    all_h[...] = value
-    out_h[rows_at(c, size_h), :] = value
-    h_copies = along("col", 9, lambda to: all_h, lambda k: out_h.at[rows_at(c, size_h)])
     gather_c.forward()
     cols.pair.forward()
     for copies in (r_copies, h_copies):

time: 150 us -> 152 us (1.013)
  Pallas kernels: 149 us -> 151 us
    pallas_call x2, Pallas kernels: 93.8 us -> 95.4 us  [middle(): pl.pallas_call(functools.partial(middle_kernel, nr, nc, first, count, gat...]
where the time goes in v4:
time: 152 us
  Pallas kernels  151 us (99%)
    pallas_call x2, Pallas kernels, middle(): pl.pallas_call(functools.partial(middle_kernel, nr, nc, first, count, gat...  95.4 us
    pallas_call x1, Pallas kernels, spread(): pl.pallas_call(functools.partial(spread_kernel, nr, nc), out_shape=tuple(...  29.1 us
    pallas_call x2, Pallas kernels, run(): pl.pallas_call(body, out_shape=tuple((jax.ShapeDtypeStruct(s, jnp.float32...  26.5 us

profile of v4, /device:TPU:1, one launch (start us, length us, event | category | flops | bytes accessed | tf_op | source)
XLA Modules:
  0.0 151.9 jit_solution(14752057049977696140)
XLA Ops:
  0.0 0.7 pad_add_fusion.pos_ref
  0.7 29.1 %spread.1 = (f32[768,128]{1,0:T(8,128)}, f32[768,128]{1,0:T(8,128)}, f32[56,128]{1,0:T(8,128)}) custom-call(f32[768,768]{1,0:T(8,128)} %a_ref.1), custom_call_target="tpu_custom_call" | custom-call | tf_op jit(solution)/shard_map/spread/pallas_call | solution.py:634
  29.8 47.9 %middle_1.1 = (f32[128,128]{1,0:T(8,128)}, f32[128,128]{1,0:T(8,128)}, f32[128,128]{1,0:T(8,128)}, f32[128,128]{1,0:T(8,128)}, f32[128,128]{1,0:T(8,128)}, /*ind...) custom-call(f32[768,768]{1,0:T(8,128)} %a_ref.1, ...), custom_call_target="tpu_custom_call" | custom-call | tf_op jit(solution)/shard_map/middle_1/pallas_call | solution.py:664
  77.7 15.5 %step_one.1 = (f32[768,768]{1,0:T(8,128)}, f32[768,128]{1,0:T(8,128)}, f32[768,128]{1,0:T(8,128)}, f32[128,128]{1,0:T(8,128)}, f32[128,128]{1,0:T(8,128)}) custom-call(s32[2]{0:T(128)} %pad_add_fusion.pos_ref, f32[128,128]{1,0:T(8,128)} %get-tuple-element.39.cinv_ref, f32[128,128]{1,0:T(8,128)} %get-tuple-element.40.rinv_ref, ...), custom_call_target="tpu_custom_call" | custom-call | tf_op jit(solution)/shard_map/step_one/pallas_call | solution.py:230
  93.2 47.5 %middle_2.1 = (f32[128,128]{1,0:T(8,128)}, f32[128,128]{1,0:T(8,128)}, f32[128,128]{1,0:T(8,128)}, f32[128,128]{1,0:T(8,128)}, f32[128,128]{1,0:T(8,128)}, /*ind...) custom-call(f32[768,768]{1,0:T(8,128)} %get-tuple-element.51.a.a_ref, ...), custom_call_target="tpu_custom_call" | custom-call | tf_op jit(solution)/shard_map/middle_2/pallas_call | solution.py:664
  140.7 11.0 %step_two.1 = f32[768,768]{1,0:T(8,128)} custom-call(s32[2]{0:T(128)} %pad_add_fusion.pos_ref, f32[128,128]{1,0:T(8,128)} %get-tuple-element.55.cinv_ref, f32[128,128]{1,0:T(8,128)} %get-tuple-element.56.rinv_ref, f32[128,128]{1,0:T(8,128)} %get-tuple-element.57.f_ref, f32[128,128]{1,0:T(8,128)} %get-tuple-element.58.ft_ref, ...), custom_call_target="tpu_custom_call" | custom-call | tf_op jit(solution)/shard_map/step_two/pallas_call | solution.py:230

commit v5 on v4

--- a/solution.py
+++ b/solution.py
@@ -21,6 +21,18 @@
     return lax.dot_general(
         left, right, (((ca,), (cb,)), ((), ())), precision=HIGH, preferred_element_type=jnp.float32
     )
+
+
+def outer(left, right):
+    def parts(x):
+        hi = x.astype(jnp.bfloat16)
+        return hi, (x - hi.astype(jnp.float32)).astype(jnp.bfloat16)
+
+    def product(x, y):
+        return lax.dot_general(x, y, (((1,), (1,)), ((), ())), preferred_element_type=jnp.float32)
+
+    (lh, ll), (rh, rl) = parts(left), parts(right)
+    return product(lh, rh) + (product(lh, rl) + product(ll, rh))
 
 
 def eliminate(x_ref, jordan):
@@ -106,7 +118,7 @@
 def step_one_kernel(
     pos_ref, cinv_ref, rinv_ref, f_ref, ft_ref, finv_ref, finvt_ref, h_ref, g_ref,
     pr_ref, sr_ref, er_ref, pc_ref, sc_ref, ec_ref, a_ref,
-    updated_ref, p2r_ref, p2c_ref, t2_ref, a33_ref, left_ref, right_ref, ht_ref, small_ref,
+    updated_ref, p2r_ref, p2c_ref, t2_ref, a33_ref, left_ref, right_ref, ht_ref, zw_ref, small_ref,
 ):
     b = BAND
     n = pr_ref.shape[0]
@@ -150,6 +162,8 @@
 
     @pl.when(always)
     def _():
+        zw_ref[:, 0:b] = small_ref[0]
+        zw_ref[:, b : 2 * b] = small_ref[1]
         t2_ref[...] = a32() - dot(small_ref[6], small_ref[1]) - dot(small_ref[5], ft_ref[...])
         a33_ref[...] = a33() - dot(small_ref[6], small_ref[2]) - dot(small_ref[5], small_ref[3])
 
@@ -163,10 +177,11 @@
             lane = lax.broadcasted_iota(jnp.int32, (tile, b), 1)
             house = dot(p_ref[at, :], rinv_ref[...]) + (ids - b == lane).astype(jnp.float32)
             cols = e_ref[at, :]
-            wk = dot(dot(s_ref[at, :], rinv_ref[...]) + cols, finvt_ref[...]) - 0.5 * dot(house, small_ref[0])
+            both = dot(house, zw_ref[...])
+            wk = dot(dot(s_ref[at, :], rinv_ref[...]) + cols, finvt_ref[...]) - 0.5 * both[:, :b]
             out_ref[at, house_at : house_at + b] = house
             out_ref[at, work_at : work_at + b] = wk
-            p2 = cols - dot(house, small_ref[1]) - dot(wk, ft_ref[...])
+            p2 = cols - both[:, b:] - dot(wk, ft_ref[...])
             p2_ref[at, :] = jnp.where(ids >= 2 * b, p2, 0.0)
 
     side(pos_ref[0], pr_ref, sr_ref, er_ref, left_ref, 0, b, p2r_ref)
@@ -175,7 +190,7 @@
     @pl.loop(0, n // tile)
     def _(step):
         at = pl.ds(pl.multiple_of(step * tile, tile), tile)
-        updated_ref[at, :] = a_ref[at, :] - mm(left_ref[at, :], right_ref[...], 1, 1)
+        updated_ref[at, :] = a_ref[at, :] - outer(left_ref[at, :], right_ref[...])
 
 
 def step_two_kernel(
@@ -217,7 +232,7 @@
     @pl.loop(0, n // tile)
     def _(step):
         at = pl.ds(pl.multiple_of(step * tile, tile), tile)
-        result_ref[at, :] = a_ref[at, :] - mm(left_ref[at, :], right_ref[...], 1, 1)
+        result_ref[at, :] = a_ref[at, :] - outer(left_ref[at, :], right_ref[...])
         store(step).start()
 
     @pl.loop(0, n // tile)
@@ -507,6 +522,8 @@
     gather_c = PairGather(r, c, nr, out_c, sems[12:])
     rows_src = lambda at: a.at[at, first * b : (first + 1) * b]
     cols_src = lambda at: xc.at[at]
+    rows.scatter(rows_src)
+    cols.scatter(cols_src)
 
     tile = 2 * b if n % (2 * b) == 0 else b
 
@@ -553,8 +570,6 @@
         )
         copy.start()
         p_copies.append(copy)
-    rows.scatter(rows_src)
-    cols.scatter(cols_src)
 
     finish(h_copies)
     value = h[rows_at(c, size_h), :]
@@ -588,6 +603,8 @@
     sum_r[...] = value
     out_r[rows_at(c, size_r), :] = value
     r_copies = along("col", 7, lambda to: sum_r, lambda k: out_r.at[rows_at(c, size_r)])
+    rows.gather(rows_src)
+    cols.gather(cols_src)
     finish(g_copies)
 
     @block
@@ -609,8 +626,6 @@
     sum_c[...] = value
     out_c[rows_at(r, size_c), :] = value
     gather_c.start(sum_c)
-    rows.gather(rows_src)
-    cols.gather(cols_src)
     finish(t_copies)
 
     @block
@@ -688,7 +703,7 @@
         step_one_kernel,
         [(n, n), (n, b), (n, b), (b, b), (b, b)],
         "step_one",
-        [vmem(n, 2 * b), vmem(n, 2 * b), vmem(b, 3 * b), vmem(7, b, b)],
+        [vmem(n, 2 * b), vmem(n, 2 * b), vmem(b, 3 * b), vmem(b, 2 * b), vmem(7, b, b)],
     )
     updated, p2r, p2c, t2, a33 = one(pos, *fac, h, t, p1r, sr, er, p1c, sc, ec, matrix)
     *fac, sr, sc, h, er, ec = middle(nr, nc, 2, 1, False, updated, p2r, p2c, t2)

time: 152 us -> 146 us (0.961)
  Pallas kernels: 151 us -> 144 us
    pallas_call x2, Pallas kernels: 95.4 us -> 89.2 us  [middle(): pl.pallas_call(functools.partial(middle_kernel, nr, nc, first, count, gat...]
where the time goes in v5:
time: 146 us; the launch traced here: 145 us
  Pallas kernels  144 us (99%)
    pallas_call x2, Pallas kernels, middle(): pl.pallas_call(functools.partial(middle_kernel, nr, nc, first, count, gat...  89.2 us
    pallas_call x1, Pallas kernels, spread(): pl.pallas_call(functools.partial(spread_kernel, nr, nc), out_shape=tuple(...  29.1 us
    pallas_call x2, Pallas kernels, run(): pl.pallas_call(body, out_shape=tuple((jax.ShapeDtypeStruct(s, jnp.float32...  25.7 us

profile of v5, /device:TPU:1, one launch (start us, length us, event | category | flops | bytes accessed | tf_op | source)
XLA Modules:
  0.0 144.8 jit_solution(11654936164552464549)
XLA Ops:
  0.0 0.7 pad_add_fusion.pos_ref
  0.7 29.1 %spread.1 = (f32[768,128]{1,0:T(8,128)}, f32[768,128]{1,0:T(8,128)}, f32[56,128]{1,0:T(8,128)}) custom-call(f32[768,768]{1,0:T(8,128)} %a_ref.1), custom_call_target="tpu_custom_call" | custom-call | tf_op jit(solution)/shard_map/spread/pallas_call | solution.py:649
  29.8 46.3 %middle_1.1 = (f32[128,128]{1,0:T(8,128)}, f32[128,128]{1,0:T(8,128)}, f32[128,128]{1,0:T(8,128)}, f32[128,128]{1,0:T(8,128)}, f32[128,128]{1,0:T(8,128)}, /*ind...) custom-call(f32[768,768]{1,0:T(8,128)} %a_ref.1, ...), custom_call_target="tpu_custom_call" | custom-call | tf_op jit(solution)/shard_map/middle_1/pallas_call | solution.py:679
  76.1 15.6 %step_one.1 = (f32[768,768]{1,0:T(8,128)}, f32[768,128]{1,0:T(8,128)}, f32[768,128]{1,0:T(8,128)}, f32[128,128]{1,0:T(8,128)}, f32[128,128]{1,0:T(8,128)}) custom-call(s32[2]{0:T(128)} %pad_add_fusion.pos_ref, f32[128,128]{1,0:T(8,128)} %get-tuple-element.39.cinv_ref, f32[128,128]{1,0:T(8,128)} %get-tuple-element.40.rinv_ref, ...), custom_call_target="tpu_custom_call" | custom-call | tf_op jit(solution)/shard_map/step_one/pallas_call | solution.py:245
  91.7 42.9 %middle_2.1 = (f32[128,128]{1,0:T(8,128)}, f32[128,128]{1,0:T(8,128)}, f32[128,128]{1,0:T(8,128)}, f32[128,128]{1,0:T(8,128)}, f32[128,128]{1,0:T(8,128)}, /*ind...) custom-call(f32[768,768]{1,0:T(8,128)} %get-tuple-element.51.a.a_ref, ...), custom_call_target="tpu_custom_call" | custom-call | tf_op jit(solution)/shard_map/middle_2/pallas_call | solution.py:679
  134.5 10.1 %step_two.1 = f32[768,768]{1,0:T(8,128)} custom-call(s32[2]{0:T(128)} %pad_add_fusion.pos_ref, f32[128,128]{1,0:T(8,128)} %get-tuple-element.55.cinv_ref, f32[128,128]{1,0:T(8,128)} %get-tuple-element.56.rinv_ref, f32[128,128]{1,0:T(8,128)} %get-tuple-element.57.f_ref, f32[128,128]{1,0:T(8,128)} %get-tuple-element.58.ft_ref, ...), custom_call_target="tpu_custom_call" | custom-call | tf_op jit(solution)/shard_map/step_two/pallas_call | solution.py:245

commit v6 on v5

--- a/solution.py
+++ b/solution.py
@@ -509,9 +509,12 @@
             copies.append(copy)
         return copies
 
+    sent = []
+
     def finish(copies):
         for copy in copies:
-            copy.wait()
+            copy.wait_recv()
+        sent.extend(copies)
 
     def block(body):
         pl.when(always)(body)
@@ -627,15 +630,17 @@
     out_c[rows_at(r, size_c), :] = value
     gather_c.start(sum_c)
     finish(t_copies)
+    cols.pair.forward()
 
     @block
     def _():
         invert_top(piece(out_t, 0) if gather else t[...], rinv, f, ft, finv, finvt)
 
     gather_c.forward()
-    cols.pair.forward()
     for copies in (r_copies, h_copies):
         finish(copies)
+    for copy in sent:
+        copy.wait_send()
     gather_c.finish()
     rows.finish(rows_src)
     cols.finish(cols_src)

time: 146 us -> 150 us (1.027)
  Pallas kernels: 144 us -> 149 us
    pallas_call x2, Pallas kernels: 89.2 us -> 94.6 us  [middle(): pl.pallas_call(functools.partial(middle_kernel, nr, nc, first, count, gat...]
where the time goes in v6:
time: 150 us
  Pallas kernels  149 us (99%)
    pallas_call x2, Pallas kernels, middle(): pl.pallas_call(functools.partial(middle_kernel, nr, nc, first, count, gat...  94.6 us
    pallas_call x1, Pallas kernels, spread(): pl.pallas_call(functools.partial(spread_kernel, nr, nc), out_shape=tuple(...  29.1 us
    pallas_call x2, Pallas kernels, run(): pl.pallas_call(body, out_shape=tuple((jax.ShapeDtypeStruct(s, jnp.float32...  25.7 us

profile of v6, /device:TPU:1, one launch (start us, length us, event | category | flops | bytes accessed | tf_op | source)
XLA Modules:
  0.0 150.2 jit_solution(8736449624686796631)
XLA Ops:
  0.0 0.7 pad_add_fusion.pos_ref
  0.7 29.1 %spread.1 = (f32[768,128]{1,0:T(8,128)}, f32[768,128]{1,0:T(8,128)}, f32[56,128]{1,0:T(8,128)}) custom-call(f32[768,768]{1,0:T(8,128)} %a_ref.1), custom_call_target="tpu_custom_call" | custom-call | tf_op jit(solution)/shard_map/spread/pallas_call | solution.py:654
  29.8 50.6 %middle_1.1 = (f32[128,128]{1,0:T(8,128)}, f32[128,128]{1,0:T(8,128)}, f32[128,128]{1,0:T(8,128)}, f32[128,128]{1,0:T(8,128)}, f32[128,128]{1,0:T(8,128)}, /*ind...) custom-call(f32[768,768]{1,0:T(8,128)} %a_ref.1, ...), custom_call_target="tpu_custom_call" | custom-call | tf_op jit(solution)/shard_map/middle_1/pallas_call | solution.py:684
  80.4 15.5 %step_one.1 = (f32[768,768]{1,0:T(8,128)}, f32[768,128]{1,0:T(8,128)}, f32[768,128]{1,0:T(8,128)}, f32[128,128]{1,0:T(8,128)}, f32[128,128]{1,0:T(8,128)}) custom-call(s32[2]{0:T(128)} %pad_add_fusion.pos_ref, f32[128,128]{1,0:T(8,128)} %get-tuple-element.39.cinv_ref, f32[128,128]{1,0:T(8,128)} %get-tuple-element.40.rinv_ref, ...), custom_call_target="tpu_custom_call" | custom-call | tf_op jit(solution)/shard_map/step_one/pallas_call | solution.py:245
  96.0 44.0 %middle_2.1 = (f32[128,128]{1,0:T(8,128)}, f32[128,128]{1,0:T(8,128)}, f32[128,128]{1,0:T(8,128)}, f32[128,128]{1,0:T(8,128)}, f32[128,128]{1,0:T(8,128)}, /*ind...) custom-call(f32[768,768]{1,0:T(8,128)} %get-tuple-element.51.a.a_ref, ...), custom_call_target="tpu_custom_call" | custom-call | tf_op jit(solution)/shard_map/middle_2/pallas_call | solution.py:684
  140.0 10.1 %step_two.1 = f32[768,768]{1,0:T(8,128)} custom-call(s32[2]{0:T(128)} %pad_add_fusion.pos_ref, f32[128,128]{1,0:T(8,128)} %get-tuple-element.55.cinv_ref, f32[128,128]{1,0:T(8,128)} %get-tuple-element.56.rinv_ref, f32[128,128]{1,0:T(8,128)} %get-tuple-element.57.f_ref, f32[128,128]{1,0:T(8,128)} %get-tuple-element.58.ft_ref, ...), custom_call_target="tpu_custom_call" | custom-call | tf_op jit(solution)/shard_map/step_two/pallas_call | solution.py:245
